TPU v7x, 128 devices: a whole 4x4x4 slice. The times are simulated.
128 devices in a mesh: lon: 16 (over y_lo, x, core), lat: 8 (over z, y_hi).
Axes of the slice: x: 4, y: 4 (y_hi: 2, y_lo: 2; y = y_hi * 2 + y_lo), z: 4, core: 2. Of those that a mesh axis runs over, the one named last changes fastest.
Arguments:
- courant_east: float32 [72, 512, 2048], P(None, 'lat', 'lon'), may hold values from -0.4 to 0.4
- courant_north: float32 [72, 512, 2048], P(None, 'lat', 'lon'), may hold values from -0.4 to 0.4
- obs_cells: int32 [8, 16, 1024], P('lat', 'lon'), may hold values from 0 to 8191
- misfit: float32 [5, 8, 16, 1024], P(None, 'lat', 'lon'), may hold values from -6 to 6
- kernel: float32 [72], replicated, may hold values from 0.25 to 1.75
- ensemble: bfloat16 [64, 512, 2048], P(None, 'lat', 'lon'), may hold values from -0.75 to 0.75
- pair_src: int32 [131072], P(('lon', 'lat')), may hold values from 0 to 4095
- pair_dst: int32 [131072], P(('lon', 'lat')), may hold values from 0 to 4095, as said below
- taper: float32 [131072], P(('lon', 'lat')), may hold values from 0.1 to 1
- var_scale: float32 [512, 2048], P('lat', 'lon'), may hold values from 0.3 to 3
Outputs:
- adjoint_field: float32 [72, 512, 2048], P(None, 'lat', 'lon')
- prior_grad: float32 [512, 2048], P('lat', 'lon')
Inputs may be any that keep to these rules, and one draw needn't show every extreme that they name: `obs_cells`: each index names a cell of its own tile. `pair_dst`: block numbers; among the 1024 pairs of one device at most 64 name blocks of one tile, and some tile gets exactly 64 of them.
All inputs are finite; a program needn't handle non-finite values.
Results may differ from a plain program's by a relative error of at most 0.004.
Values sent between devices are 32-bit elements; how exact they have to be, the bound alone decides.
A program may use at most 128 MiB of HBM per device.

v0:
```python
import jax
import jax.numpy as jnp
from jax import lax
from jax.sharding import PartitionSpec as P

BLK = 16


def passed_along(block, axis, distance):
    devices = range(lax.axis_size(axis))
    route = [((i - distance) % len(devices), i) for i in devices]
    return lax.ppermute(block, axis, route)


def from_behind(value, axis, steps):
    count = lax.axis_size(axis)
    initial, last = (max(0, -steps), min(count, count - steps))
    return lax.ppermute(value, axis, [(source, source + steps) for source in range(initial, last)])


def with_halo(block, sides, width):
    for axis, dim in sides:
        count = lax.axis_size(axis)
        forward = [(i, i + 1) for i in range(count - 1)]
        forward.append((count - 1, 0))
        backward = [(target, source) for source, target in forward]
        low = lax.ppermute(
            lax.slice_in_dim(block, block.shape[dim] - width, None, axis=dim), axis, forward
        )
        high = lax.ppermute(lax.slice_in_dim(block, 0, width, axis=dim), axis, backward)
        block = jnp.concatenate([low, block, high], axis=dim)
    return block


def per_device(
    courant_east,
    courant_north,
    obs_cells,
    misfit,
    kernel,
    ensemble,
    pair_src,
    pair_dst,
    taper,
    var_scale,
):
    levels, tile_lat, tile_lon = courant_east.shape
    lat_count = lax.axis_size("lat")
    lon_count = lax.axis_size("lon")
    rows_global = lax.axis_index("lat") * tile_lat + jnp.arange(tile_lat, dtype=jnp.int32)
    keep_rows = (rows_global < tile_lat * lat_count - 1)[None, :, None]
    north_face = jnp.where(keep_rows, courant_north, 0.0)
    pos_east = jnp.maximum(courant_east, 0.0)
    pos_north = jnp.maximum(north_face, 0.0)
    neg_east = jnp.minimum(courant_east, 0.0)
    neg_north = jnp.minimum(north_face, 0.0)
    west_column = passed_along(neg_east[:, :, -1:], "lon", 1)
    neg_west = jnp.concatenate([west_column, neg_east[:, :, :-1]], axis=2)
    south_row = from_behind(neg_north[:, -1:, :], "lat", 1)
    neg_south = jnp.concatenate([south_row, neg_north[:, :-1, :]], axis=1)
    flat_cells = obs_cells.reshape(-1)

    def forcing(step_index):
        column = (
            jnp.zeros((tile_lat * tile_lon,), jnp.float32)
            .at[flat_cells]
            .add(misfit[step_index].reshape(-1))
        )
        return kernel[:, None, None] * column.reshape(tile_lat, tile_lon)[None]

    adj_field = forcing(0)
    surface = adj_field[0]
    for step_index in range(1, misfit.shape[0]):
        padded = with_halo(adj_field, (("lat", 1), ("lon", 2)), 1)
        east_vals = padded[:, 1:-1, 2:]
        west_vals = padded[:, 1:-1, :-2]
        north_vals = padded[:, 2:, 1:-1]
        south_vals = padded[:, :-2, 1:-1]
        adj_field = (
            adj_field
            + pos_east * (east_vals - adj_field)
            + neg_west * (adj_field - west_vals)
            + pos_north * (north_vals - adj_field)
            + neg_south * (adj_field - south_vals)
            + forcing(step_index)
        )
        surface = surface + adj_field[0]
    members = ensemble.shape[0]
    block_rows = tile_lat // BLK
    block_cols = tile_lon // BLK
    own_blocks = block_rows * block_cols
    ens_blocks = ensemble.reshape(members, block_rows, BLK, block_cols, BLK)
    grad_blocks = surface.astype(jnp.bfloat16).reshape(block_rows, BLK, block_cols, BLK)
    local_coeffs = jnp.einsum(
        "mrpcq,rpcq->rcm", ens_blocks, grad_blocks, preferred_element_type=jnp.float32
    ).reshape(own_blocks, members)
    device_count = lon_count * lat_count
    total_blocks = own_blocks * device_count
    all_coeffs = lax.all_gather(local_coeffs, ("lon", "lat"), axis=0, tiled=True)
    partial_sums = jax.ops.segment_sum(
        taper[:, None] * all_coeffs[pair_src], pair_dst, num_segments=total_blocks
    )
    combined = lax.psum_scatter(partial_sums, ("lon", "lat"), scatter_dimension=0, tiled=True)
    combined16 = combined.astype(jnp.bfloat16).reshape(block_rows, block_cols, members)
    field_part = jnp.einsum(
        "mrpcq,rcm->rpcq", ens_blocks, combined16, preferred_element_type=jnp.float32
    ).reshape(tile_lat, tile_lon)
    prior_grad = var_scale * surface + field_part
    return (adj_field, prior_grad)


def solution(mesh):
    in_specs = (
        P(None, "lat", "lon"),
        P(None, "lat", "lon"),
        P("lat", "lon", None),
        P(None, "lat", "lon", None),
        P(),
        P(None, "lat", "lon"),
        P(("lon", "lat")),
        P(("lon", "lat")),
        P(("lon", "lat")),
        P("lat", "lon"),
    )
    out_specs = (P(None, "lat", "lon"), P("lat", "lon"))
    return jax.shard_map(
        per_device, mesh=mesh, in_specs=in_specs, out_specs=out_specs, check_vma=False
    )
```

profile of v0, /device:TPU:1, one launch (start us, length us, event | category | flops | bytes accessed | tf_op | source)
XLA Modules:
  0.0 1178.9 jit_solution(14152861951485718959)
XLA Ops:
  7.2 1.3 fusion.79
  9.3 5.9 scatter_custom_fusion
  15.2 0.9 broadcast_multiply_fusion
  16.1 1.4 copy-done.3
  17.5 3.8 collective-permute-start
  21.3 3.6 collective-permute-start.1
  24.9 2.2 select_minimum_fusion
  27.1 1.3 collective-permute-start.5
  28.9 3.1 fusion.74
  32.0 2.5 copy.20
  34.6 1.6 collective-permute-start.2
  36.1 2.5 copy.24
  38.7 1.2 collective-permute-start.4
  39.8 1.9 broadcast_minimum_fusion
  41.7 1.4 copy-done.5
  43.1 2.1 slice.205
  45.2 2.8 copy.22
  48.6 6.5 scatter_custom_fusion.1
  55.0 3.2 copy.23
  58.2 2.4 copy.21
  60.6 2.4 copy.25
  63.0 12.2 %fusion.4 = (f32[72,64,128]{2,1,0:T(8,128)S(1)}, f32[72,64,128]{2,1,0:T(8,128)}) fusion(f32[72,64,128]{2,1,0:T(8,128)} %copy-done.3, f32[72,1,128]{2,1,0:T(1,128)S(1)} %collective-permute-done, f32[72,1,128]{2,1,0:T(1,128)S(1)} %collective-permute-done.1, f32[72,66,1]{2,1,0:T(8,128)} %copy.25, f32[72,66,1]{2,1,0:T(8,128)} %copy.21, ...), kind=kLoop, calls=%fused_computation.20 | loop fusion | flops 16515072 | bytes 16692704 | tf_op jit(solution)/shard_map/add | solution.py:80
  75.2 2.4 collective-permute-start.6
  77.6 2.8 collective-permute-start.7
  80.4 1.3 collective-permute-done.6
  82.7 3.1 fusion.73
  85.8 2.5 copy.26
  88.3 2.6 collective-permute-start.8
  90.9 2.5 copy.28
  93.5 6.1 scatter_custom_fusion.2
  99.7 2.4 copy.27
  102.1 2.4 copy.29
  104.4 10.6 fusion.37
  115.1 2.7 collective-permute-start.10
  117.8 2.5 collective-permute-start.11
  120.2 1.3 collective-permute-done.10
  122.5 3.1 fusion.72
  125.7 2.5 copy.30
  128.2 3.4 collective-permute-start.12
  131.6 2.5 copy.32
  134.2 5.9 scatter_custom_fusion.3
  140.1 2.4 copy.31
  142.5 2.4 copy.33
  144.9 11.0 fusion.24
  156.0 2.8 collective-permute-start.14
  158.8 2.6 collective-permute-start.15
  161.3 1.3 collective-permute-done.14
  163.5 3.2 fusion.71
  166.7 3.2 copy.34
  169.9 4.4 collective-permute-start.16
  174.4 3.1 copy.36
  177.5 6.1 scatter_custom_fusion.4
  183.6 2.3 copy.38
  185.9 3.1 copy.35
  189.0 3.2 copy.37
  192.2 10.8 fusion.11
  203.0 1.4 copy-done.7
  204.4 0.8 fusion.70
  205.3 2.8 fusion.49
  208.5 304.7 %all-gather.2.cloned.1.call-done = f32[4096,64]{1,0:T(8,128)} async-done(((f32[32,64]{1,0:T(8,128)}), f32[4096,64]{1,0:T(8,128)}) %all-gather.2.cloned.1.call-update) | async-done | bytes 1048592 | tf_op jit(solution)/shard_map/all_gather | solution.py:99
  513.2 13.8 %scatter_custom_fusion.5 = f32[4096,64]{1,0:T(8,128)} fusion(s32[1024]{0:T(1024)} %param.17, f32[]{:T(128)} %constant.7.clone.1, f32[1024]{0:T(1024)S(1)} %copy-done.14, f32[4096,64]{1,0:T(8,128)} %all-gather.2.cloned.1.call-done, s32[1024]{0:T(1024)S(1)} %fusion.68), kind=kCustom, calls=%fused_computation.105 | custom fusion | flops 131072 | bytes 3154432 | tf_op jit(solution)/shard_map/scatter-add | solution.py:100
  527.0 638.0 %reduce-scatter.2.cloned.1.call-done = f32[32,64]{1,0:T(8,128)} async-done(((f32[4096,64]{1,0:T(8,128)}), f32[32,64]{1,0:T(8,128)}) %reduce-scatter.2.cloned.1.call-update) | async-done | bytes 8208 | tf_op jit(solution)/shard_map/reduce_scatter | solution.py:103
  1165.1 0.7 convert_bitcast_fusion
  1165.8 4.9 fusion.47
  (66 shorter events, 6.1 us)
Async XLA Ops:
  7.2 506.0 %all-gather.2.cloned.1.call-start = ((), (), s32[]{:S(2)}) async-start(), calls=%async_computation.1 | async-start | bytes 2113536 | tf_op jit(solution)/shard_map/all_gather | solution.py:99
  9.2 124.9 %copy-start.13 = (s32[1024,1]{0,1:T(1,128)}, s32[1024,1]{0,1:T(1,128)S(1)}, u32[]{:S(2)}) copy-start(s32[1024,1]{0,1:T(1,128)S(1)} %compare_select_fusion) | copy-start | bytes 12292
  16.1 1.4 copy-start.3
  17.5 10.9 collective-permute-start
  21.3 7.1 collective-permute-start.1
  24.9 3.6 copy-start.4
  27.1 35.9 %collective-permute-start.5 = (f32[72,1,128]{2,1,0:T(1,128)S(1)}, f32[72,1,128]{2,1,0:T(1,128)S(1)}, u32[]{:S(2)}, u32[]{:S(2)}) collective-permute-start(f32[72,1,128]{2,1,0:T(1,128)S(1)} %slice.208), channel_id=1, source_target_pairs={{0,1},{1,2},{2,3},{3,4},{4,5},{5,6},{6,7},{8,9},{9,10},{10,11},{11... | collective-permute-start | bytes 110600 | tf_op jit(solution)/shard_map/ppermute | solution.py:18
  34.6 23.6 %collective-permute-start.2 = (f32[72,66,1]{0,2,1:T(1,128)S(1)}, f32[72,66,1]{0,2,1:T(1,128)S(1)}, u32[]{:S(2)}, u32[]{:S(2)}) collective-permute-start(f32[72,66,1]{0,2,1:T(1,128)S(1)} %copy.20), channel_id=1, source_target_pairs={{8,0},{16,8},{24,16},{32,24},{40,32},{48,40},{56,48},{64,56},{72,6... | collective-permute-start | bytes 57032 | tf_op jit(solution)/shard_map/ppermute | solution.py:30
  38.7 22.0 %collective-permute-start.4 = (f32[72,66,1]{0,2,1:T(1,128)S(1)}, f32[72,66,1]{0,2,1:T(1,128)S(1)}, u32[]{:S(2)}, u32[]{:S(2)}) collective-permute-start(f32[72,66,1]{0,2,1:T(1,128)S(1)} %copy.24), channel_id=1, source_target_pairs={{0,8},{8,16},{16,24},{24,32},{32,40},{40,48},{48,56},{56,64},{64,7... | collective-permute-start | bytes 57032 | tf_op jit(solution)/shard_map/ppermute | solution.py:27
  41.7 1.4 copy-start.5
  48.0 7.0 collective-permute-start.3
  58.2 4.8 copy-start.10
  75.2 7.5 copy-start
  75.2 6.5 collective-permute-start.6
  77.6 4.6 collective-permute-start.7
  88.3 11.3 collective-permute-start.8
  93.5 8.6 collective-permute-start.9
  115.0 7.5 copy-start.1
  115.1 6.5 collective-permute-start.10
  117.8 4.3 collective-permute-start.11
  128.2 11.9 %collective-permute-start.12 = (f32[72,66,1]{0,2,1:T(1,128)S(1)}, f32[72,66,1]{0,2,1:T(1,128)S(1)}, u32[]{:S(2)}, u32[]{:S(2)}) collective-permute-start(f32[72,66,1]{0,2,1:T(1,128)S(1)} %copy.30), channel_id=1, source_target_pairs={{8,0},{16,8},{24,16},{32,24},{40,32},{48,40},{56,48},{64,56},{72,6... | collective-permute-start | bytes 57032 | tf_op jit(solution)/shard_map/ppermute | solution.py:30
  134.1 8.4 collective-permute-start.13
  155.9 7.6 copy-start.2
  156.0 6.7 collective-permute-start.14
  158.8 4.3 collective-permute-start.15
  166.7 16.9 %copy-start.8 = (bf16[64,64,128]{2,1,0:T(8,128)(2,1)S(1)}, bf16[64,64,128]{2,1,0:T(8,128)(2,1)}, u32[]{:S(2)}) copy-start(bf16[64,64,128]{2,1,0:T(8,128)(2,1)} %param.15) | copy-start | bytes 3145732
  169.9 16.0 %collective-permute-start.16 = (f32[72,66,1]{0,2,1:T(1,128)}, f32[72,66,1]{0,2,1:T(1,128)}, u32[]{:S(2)}, u32[]{:S(2)}) collective-permute-start(f32[72,66,1]{0,2,1:T(1,128)} %copy.34), channel_id=1, source_target_pairs={{8,0},{16,8},{24,16},{32,24},{40,32},{48,40},{56,48},{64,56},{72,6... | collective-permute-start | bytes 57032 | tf_op jit(solution)/shard_map/ppermute | solution.py:30
  177.5 11.5 collective-permute-start.17
  185.9 6.3 copy-start.11
  202.9 1.4 copy-start.7
  204.4 4.1 copy-start.12
  204.4 308.8 %copy-start.14 = (f32[1024]{0:T(1024)S(1)}, f32[1024]{0:T(1024)}, u32[]{:S(2)}) copy-start(f32[1024]{0:T(1024)} %param.18) | copy-start | bytes 12292
  208.2 956.9 %reduce-scatter.2.cloned.1.call-start = ((), (), s32[]{:S(2)}) async-start(), calls=%async_computation.2 | async-start | bytes 2113536 | tf_op jit(solution)/shard_map/reduce_scatter | solution.py:103
  208.5 957.3 %copy-start.6 = (bf16[64,64,128]{0,2,1:T(8,128)(2,1)S(1)}, bf16[64,64,128]{0,2,1:T(8,128)(2,1)}, u32[]{:S(2)}) copy-start(bf16[64,64,128]{0,2,1:T(8,128)(2,1)} %copy.38) | copy-start | bytes 3145732
  527.0 644.0 %copy-start.9 = (f32[64,128]{1,0:T(8,128)S(1)}, f32[64,128]{1,0:T(8,128)}, u32[]{:S(2)}) copy-start(f32[64,128]{1,0:T(8,128)} %param.19) | copy-start | bytes 98308
Sparse Core Ops, SparseCore 0:
  208.3 304.8 all-gather.1
  527.2 637.8 reduce-scatter.1
where the time goes:
time: 1200 us; the launch traced here: 1180 us
  waiting for transfers between devices  948 us (79%)
  other arithmetic  98.3 us (8%)
  local copies, waits for them, and re-layouts  71.3 us (6%)
  starting transfers between devices  38.5 us (3%)
  between operations  14.9 us (1%)
    reduce_scatter x1, waiting for transfers between devices, per_device(): lax.psum_scatter(partial_sums, ('lon', 'lat'), scatter_dimension=0, tiled...  638 us
    all_gather x1, waiting for transfers between devices, per_device(): lax.all_gather(local_coeffs, ('lon', 'lat'), axis=0, tiled=True)  305 us
    add x4, other arithmetic, per_device(): adj_field + pos_east * (east_vals - adj_field)  44.5 us
    scatter-add x5, other arithmetic, forcing(): column = jnp.zeros((tile_lat * tile_lon,), jnp.float32).at[flat_cells].ad...  30.5 us
  transfers between devices with their start and end apart: 20, of which 8 were waited for; matrix products, arithmetic and copies ran while one was open for 6% of the time, Pallas kernels for 0%

commit v1 on v0

v1 whole, which is shorter than its diff:
```python
import functools

import jax
import jax.numpy as jnp
from jax import lax
from jax.experimental import pallas as pl
from jax.experimental.pallas import tpu as pltpu
from jax.sharding import PartitionSpec as P

MESH = pl.DeviceIdType.MESH
F32, BF16, I32 = jnp.float32, jnp.bfloat16, jnp.int32

TLAT, TLON, LEV, BLK, MEM = 64, 128, 72, 16, 64
NLON, NLAT = 16, 8
FIELDS = 5
EXT = 7
ROWS = TLAT + 16
GROUPS = 3
KG = LEV // GROUPS
ROUNDS = 3
CHUNKS = 8
COPIES = 8 + 2 + 4 * ROUNDS * GROUPS + 15 + 7 + 1 + 9 + 9


def iota(shape, dim):
    return lax.broadcasted_iota(I32, shape, dim)


def dot_nt(a, b):
    return lax.dot_general(a, b, (((1,), (1,)), ((), ())), preferred_element_type=F32)


def dot_tn(a, b):
    return lax.dot_general(a, b, (((0,), (0,)), ((), ())), preferred_element_type=F32)


def dot_nn(a, b):
    return lax.dot_general(a, b, (((1,), (0,)), ((), ())), preferred_element_type=F32)


def parts_of(x, count):
    parts = []
    for _ in range(count):
        part = x.astype(BF16)
        parts.append(part)
        x = x - part.astype(F32)
    return parts


def kernel(
    ce_hbm, cn_hbm, cells, misfit, kern, ens_hbm, psrc, pdst, taper, var_ref,
    out_hbm, prior_ref,
    ce, cn, aw, asn, c0, field, last, ens, area, halo_e, halo_w, pack_e, pack_w,
    cpack, chalo, crow, crhalo, shifted,
    fpack_e, fpack_w, fhalo_e, fhalo_w, frow_n, frow_s, frhalo_n, frhalo_s,
    slots1, route1, slots2, route2, lhs, rhs, weights,
    partial, own, table, ycol,
    local_sem, out_sem, send_sem, recv_sem,
):
    lon, lat = lax.axis_index("lon"), lax.axis_index("lat")
    core, x, y_lo = lon % 2, (lon // 2) % 4, lon // 8
    z, y_hi = lat // 2, lat % 2
    y = y_hi * 2 + y_lo

    def shift_lon(s):
        return (lon + s + NLON) % NLON

    def shift_lat(s):
        return (lat + s + NLAT) % NLAT

    def device(xx, yy, zz, cc):
        return {"lon": (yy % 2) * 8 + xx * 2 + cc, "lat": zz * 2 + yy // 2}

    ce_in = pltpu.make_async_copy(ce_hbm, ce, local_sem.at[0])
    cn_in = pltpu.make_async_copy(cn_hbm, cn.at[:, pl.ds(8, TLAT), :], local_sem.at[1])
    ens_in = pltpu.make_async_copy(ens_hbm, ens, local_sem.at[2])
    ce_in.start()
    cn_in.start()
    ens_in.start()

    barrier = pltpu.get_barrier_semaphore()
    peers = [{"lon": shift_lon(i), "lat": lat} for i in range(1, NLON)]
    peers += [{"lon": lon, "lat": shift_lat(i)} for i in range(1, NLAT)]
    peers += [device(x, (y + i) % 4, z, core) for i in (1, 3)]
    peers += [{"lon": shift_lon(i), "lat": shift_lat(j)} for i in (-1, 1) for j in (-1, 1)]
    for peer in peers:
        pl.semaphore_signal(barrier, inc=1, device_id=peer, device_id_type=MESH)

    used = [0]

    def remote(src, dst, peer):
        n = used[0]
        used[0] += 1
        return pltpu.make_async_remote_copy(
            src_ref=src, dst_ref=dst, send_sem=send_sem.at[n], recv_sem=recv_sem.at[n],
            device_id=peer, device_id_type=MESH,
        )

    lane = iota((TLAT, TLON), 1)

    columns = [jnp.zeros((TLAT, TLON), F32) for _ in range(FIELDS)]
    for q in range(CHUNKS):
        cell = cells[q : q + 1, :]
        in_row = iota((TLAT, 128), 0) == cell // TLON
        in_col = jnp.where(iota((TLON, 128), 0) == cell % TLON, 1.0, 0.0).astype(BF16)
        weighted = []
        for t in range(FIELDS):
            value = misfit[t, q : q + 1, :]
            for part in parts_of(value, 2):
                weighted.append(jnp.where(in_row, part.astype(F32), 0.0).astype(BF16))
        placed = dot_nt(jnp.concatenate(weighted, axis=0), in_col)
        for t in range(FIELDS):
            base = 2 * t * TLAT
            columns[t] += placed[base : base + TLAT] + placed[base + TLAT : base + 2 * TLAT]
    for t in range(FIELDS):
        area[t, 8 : 8 + TLAT, :] = columns[t]

    total = jnp.zeros((128, 128), F32)
    slot1 = jnp.zeros((128, 128), F32)
    slot2 = jnp.zeros((128, 128), F32)
    before = jnp.where(iota((128, 128), 0) < iota((128, 128), 1), 1.0, 0.0).astype(BF16)
    ones = jnp.ones((128, 128), BF16)
    for q in range(CHUNKS):
        src, dst, weight = psrc[q : q + 1, :], pdst[q : q + 1, :], taper[q : q + 1, :]
        mine = iota((128, 128), 0) == dst // 32
        mark = jnp.where(mine, 1.0, 0.0).astype(BF16)
        count = dot_nn(mark, before) + total
        total += dot_nn(mark, ones)
        rank = jnp.sum(jnp.where(mine, count, 0.0), axis=0, keepdims=True).astype(I32)
        at_low = jnp.where(iota((128, 128), 0) == rank, 1.0, 0.0).astype(BF16)
        at_high = jnp.where(iota((128, 128), 0) == rank + 64, 1.0, 0.0).astype(BF16)
        s_tile, s_row, s_col = src // 32, (src // 8) % 4, src % 8
        s_lon, s_lat = s_tile // 8, s_tile % 8
        s_core, s_x, s_y, s_z = s_lon % 2, (s_lon // 2) % 4, (s_lat % 2) * 2 + s_lon // 8, s_lat // 2
        s_slot = jnp.where(s_core == 0, s_z * 16 + s_y * 4 + s_x, s_x * 16 + s_z * 4 + s_y)
        where_src = s_core * 512 + s_slot * 8 + s_col
        key1 = (where_src // 256) * 128 + s_row * 32 + dst % 32
        key2 = where_src % 256

        def spread(value):
            return jnp.where(mine, value, 0.0).astype(BF16)

        high, low = (key1 // 2 * 2).astype(F32), (key1 % 2).astype(F32)
        slot1 += dot_nt(spread(high), at_low) + dot_nt(spread(low), at_low)
        slot1 += dot_nt(spread(key2.astype(F32)), at_high)
        for part in parts_of(weight, 2):
            slot2 += dot_nt(spread(part.astype(F32)), at_low)
    for d in range(NLON):
        slots1[d, 0] = slot1[d * 8 : d * 8 + 8]
        slots1[d, 1] = slot2[d * 8 : d * 8 + 8]

    ce_in.wait()
    cn_in.wait()
    area[5, 8 : 8 + TLAT, :] = ce[0]
    area[6, 8 : 8 + TLAT, :] = cn[0, 8 : 8 + TLAT, :]
    first = jnp.zeros((TLAT, TLON), F32)
    final = jnp.zeros((TLAT, TLON), F32)
    for n in range(EXT):
        value = area[n, 8 : 8 + TLAT, :]
        here = (lane >= 4 * n) & (lane < 4 * n + 4)
        first = jnp.where(here, pltpu.roll(value, 4 * n, 1) if n else value, first)
        final = jnp.where(here, pltpu.roll(value, 4 * n + 4, 1), final)
    pack_w[...] = first
    pack_e[...] = final

    def pack_courant(k, acc):
        return jnp.where(lane == k, pltpu.roll(ce[k], k + 1, 1), acc)

    cpack[...] = lax.fori_loop(0, LEV, pack_courant, jnp.zeros((TLAT, TLON), F32))
    cn_rows = cn.reshape(LEV * (TLAT + 8), TLON)
    crow[...] = cn_rows[pl.ds(TLAT + 7, LEV, stride=TLAT + 8), :]

    pl.semaphore_wait(barrier, len(peers))

    east = {"lon": shift_lon(1), "lat": lat}
    west = {"lon": shift_lon(-1), "lat": lat}
    north = {"lon": lon, "lat": shift_lat(1)}
    south = {"lon": lon, "lat": shift_lat(-1)}
    mid, low8, high8 = pl.ds(8, TLAT), pl.ds(0, 8), pl.ds(TLAT + 8, 8)
    edges = [
        remote(area.at[:, pl.ds(TLAT, 8), :], area.at[:, low8, :], north),
        remote(area.at[:, pl.ds(8, 8), :], area.at[:, high8, :], south),
        remote(pack_e.at[pl.ds(TLAT - 8, 8), :], halo_w.at[low8, :], {"lon": shift_lon(1), "lat": shift_lat(1)}),
        remote(pack_e.at[pl.ds(0, 8), :], halo_w.at[high8, :], {"lon": shift_lon(1), "lat": shift_lat(-1)}),
        remote(pack_w.at[pl.ds(TLAT - 8, 8), :], halo_e.at[low8, :], {"lon": shift_lon(-1), "lat": shift_lat(1)}),
        remote(pack_w.at[pl.ds(0, 8), :], halo_e.at[high8, :], {"lon": shift_lon(-1), "lat": shift_lat(-1)}),
        remote(pack_e, halo_w.at[mid, :], east),
        remote(pack_w, halo_e.at[mid, :], west),
    ]
    courants = [remote(crow, crhalo, north), remote(cpack, chalo, east)]
    routes = [
        remote(slots1.at[shift_lon(i)], route1.at[lon], {"lon": shift_lon(i), "lat": lat})
        for i in range(1, NLON)
    ]
    for copy in edges + courants + routes:
        copy.start()

    for copy in edges:
        copy.wait_recv()

    wide_lane = iota((ROWS, TLON), 1)

    def widened(n):
        from_east = halo_e[...] if n == 0 else pltpu.roll(halo_e[...], 128 - 4 * n, 1)
        from_west = pltpu.roll(halo_w[...], 124 - 4 * n, 1)
        side = jnp.where(wide_lane < 64, from_east, from_west)
        return jnp.concatenate([area[n], side], axis=1)

    def up(v, axis):
        return pltpu.roll(v, v.shape[axis] - 1, axis)

    def down(v, axis):
        return pltpu.roll(v, 1, axis)

    forced = [widened(t) for t in range(FIELDS)]
    east0 = widened(5)
    global_row = lat * TLAT - 8 + iota((ROWS, 2 * TLON), 0)
    inside = (global_row >= 0) & (global_row < NLAT * TLAT - 1)
    north0 = jnp.where(inside, widened(6), 0.0)
    pe0, pn0 = jnp.maximum(east0, 0.0), jnp.maximum(north0, 0.0)
    aw0, as0 = -jnp.minimum(down(east0, 1), 0.0), -jnp.minimum(down(north0, 0), 0.0)
    c00 = 1.0 - pe0 - aw0 - pn0 - as0
    k0 = kern[0]
    level = k0 * forced[0]
    surface_wide = level
    for t in range(1, FIELDS):
        level = (
            c00 * level + pe0 * up(level, 1) + aw0 * down(level, 1)
            + pn0 * up(level, 0) + as0 * down(level, 0) + k0 * forced[t]
        )
        surface_wide = surface_wide + level
    surface = surface_wide[8 : 8 + TLAT, :TLON]
    prior_ref[...] = surface
    base = forced[0]
    for n, v in enumerate((base, up(base, 1), down(base, 1), up(base, 0), down(base, 0))):
        shifted[n] = v[8 : 8 + TLAT, :TLON]

    ens_in.wait()
    rounded = surface.astype(BF16).astype(F32)

    @pl.loop(0, MEM)
    def _(m):
        product = ens[m].astype(F32) * rounded
        for r in range(4):
            at = pl.multiple_of((r * MEM + m) * 8, 8)
            partial[pl.ds(at, 8), :] = product[r * 16 : r * 16 + 8] + product[r * 16 + 8 : r * 16 + 16]

    row_sums = partial[pl.ds(0, 256, stride=8), :]
    for s in range(1, 8):
        row_sums += partial[pl.ds(s, 256, stride=8), :]
    in_block = jnp.where(iota((8, TLON), 0) == iota((8, TLON), 1) // BLK, 1.0, 0.0).astype(BF16)
    own[...] = sum(dot_nt(in_block, part) for part in parts_of(row_sums, 3))

    slot = jnp.where(core == 0, z * 16 + y * 4 + x, x * 16 + z * 4 + y)
    sibling = device(x, y, z, 1 - core)
    moves = [(1 - core, core, 0), (0, 1 - core, core), (core, 0, 1 - core)]

    def ring_peer(phase, s):
        dx, dy, dz = moves[phase]
        return device((x + s * dx) % 4, (y + s * dy) % 4, (z + s * dz) % 4, core)

    def gather_sends(phase):
        if phase == 0:
            src, dst = own, table.at[core, slot]
        else:
            size = 4**phase
            first_slot = slot // size * size
            src = table.at[core, pl.ds(first_slot, size)]
            dst = table.at[core, pl.ds(first_slot, size)]
        return [remote(src, dst, ring_peer(phase, s)) for s in (2, 1, 3)]

    def share_sends(phase):
        size = 4**phase
        group = slot // (4 * size) * (4 * size)
        place = slot // size % 4
        copies = []
        for s in (1, 3, 2):
            rows = pl.ds(group + (place + s) % 4 * size, size)
            copies.append(remote(table.at[core, rows], table.at[core, rows], sibling))
        return copies

    shares = [remote(own, table.at[core, slot], sibling)]
    gathers = [gather_sends(0)]
    for copy in gathers[0] + shares:
        copy.start()
    table[core, slot] = own[...]

    def next_phase(phase):
        for copy in gathers[phase]:
            copy.wait_recv()
        if phase < 2:
            gathers.append(gather_sends(phase + 1))
            for copy in gathers[phase + 1]:
                copy.start()
        more = share_sends(phase)
        for copy in more:
            copy.start()
        shares.extend(more)

    for copy in courants:
        copy.wait_recv()
    cn_rows[pl.ds(7, LEV, stride=TLAT + 8), :] = crhalo[...] * jnp.where(lat > 0, 1.0, 0.0)
    field_rows = field.reshape(LEV * ROWS, TLON)
    keep = lat * TLAT + iota((TLAT, TLON), 0) < NLAT * TLAT - 1

    def step(t, g, k, carry):
        kk = kern[k]
        if t == 1:
            faces = ce[k]
            pe = jnp.maximum(faces, 0.0)
            behind = jnp.where(lane == 0, pltpu.roll(chalo[...], (128 - k) % 128, 1), pltpu.roll(faces, 1, 1))
            w = -jnp.minimum(behind, 0.0)
            pn = jnp.where(keep, jnp.maximum(cn[k, 8 : 8 + TLAT, :], 0.0), 0.0)
            s = -jnp.minimum(cn[k, 7 : 7 + TLAT, :], 0.0)
            c = 1.0 - pe - w - pn - s
            ce[k] = pe
            cn[k, 8 : 8 + TLAT, :] = pn
            aw[k], asn[k], c0[k] = w, s, c
            new = kk * (
                c * shifted[0] + pe * shifted[1] + w * shifted[2] + pn * shifted[3] + s * shifted[4]
                + area[1, 8 : 8 + TLAT, :]
            )
        else:
            here = field[k, 8 : 8 + TLAT, :]
            j = k - g * KG
            to_east = jnp.where(lane == 127, pltpu.roll(fhalo_e[t - 2, g], 127 - j, 1), pltpu.roll(here, 127, 1))
            to_west = jnp.where(lane == 0, pltpu.roll(fhalo_w[t - 2, g], (128 - j) % 128, 1), pltpu.roll(here, 1, 1))
            new = (
                c0[k] * here + ce[k] * to_east + aw[k] * to_west
                + cn[k, 8 : 8 + TLAT, :] * field[k, 9 : 9 + TLAT, :]
                + asn[k] * field[k, 7 : 7 + TLAT, :] + kk * area[t, 8 : 8 + TLAT, :]
            )
        if t == 4:
            last[k] = new
            return carry
        field[k, 8 : 8 + TLAT, :] = new
        j = k - g * KG
        first, final = carry
        first = jnp.where(lane == j, pltpu.roll(new, j, 1), first)
        final = jnp.where(lane == j, pltpu.roll(new, j + 1, 1), final)
        return first, final

    sent = {}
    outs = []

    def run_step(t):
        zeros = jnp.zeros((TLAT, TLON), F32)
        for g in range(GROUPS):
            start = g * KG * ROWS
            if t > 1:
                for copy in sent[t - 1, g]:
                    copy.wait_recv()
                field_rows[pl.ds(start + 7, KG, stride=ROWS), :] = frhalo_s[t - 2, g]
                field_rows[pl.ds(start + 8 + TLAT, KG, stride=ROWS), :] = frhalo_n[t - 2, g]
            if t == 4:
                lax.fori_loop(g * KG, (g + 1) * KG, functools.partial(step, t, g), 0)
                levels = pl.ds(g * KG, KG)
                outs.append(pltpu.make_async_copy(last.at[levels], out_hbm.at[levels], out_sem.at[g]))
                outs[-1].start()
                continue
            first, final = lax.fori_loop(
                g * KG, (g + 1) * KG, functools.partial(step, t, g), (zeros, zeros)
            )
            fpack_w[t - 1, g] = first
            fpack_e[t - 1, g] = final
            frow_n[t - 1, g] = field_rows[pl.ds(start + 7 + TLAT, KG, stride=ROWS), :]
            frow_s[t - 1, g] = field_rows[pl.ds(start + 8, KG, stride=ROWS), :]
            sent[t, g] = [
                remote(frow_n.at[t - 1, g], frhalo_s.at[t - 1, g], north),
                remote(frow_s.at[t - 1, g], frhalo_n.at[t - 1, g], south),
                remote(fpack_e.at[t - 1, g], fhalo_w.at[t - 1, g], east),
                remote(fpack_w.at[t - 1, g], fhalo_e.at[t - 1, g], west),
            ]
            for copy in sent[t, g]:
                copy.start()

    run_step(1)

    next_phase(0)

    route1[lon] = slots1[lon]
    for copy in routes:
        copy.wait_recv()
    for n in range(2):
        for a in range(NLAT):
            slots2[a, n] = jnp.concatenate([route1[d, n, a : a + 1, :] for d in range(NLON)], axis=0)
    routes2 = [
        remote(slots2.at[shift_lat(i)], route2.at[lat], {"lon": lon, "lat": shift_lat(i)})
        for i in range(1, NLAT)
    ]
    for copy in routes2:
        copy.start()
    route2[lat] = slots2[lat]

    run_step(2)

    next_phase(1)

    for copy in routes2:
        copy.wait_recv()
    half = iota((16, 128), 1) < 64

    for a in range(4):
        one, two = route2[a, 0], route2[a + 4, 0]
        key1 = jnp.where(half, one, pltpu.roll(two, 64, 1)).astype(I32)
        key2 = jnp.where(half, pltpu.roll(one, 64, 1), two).astype(I32)
        weight = jnp.where(half, route2[a, 1], pltpu.roll(route2[a + 4, 1], 64, 1))
        for q in range(2):
            for i in range(8):
                r = q * 8 + i
                cols = slice(i * 128, (i + 1) * 128)
                lhs[:, cols] = jnp.where(iota((512, 128), 0) == key1[r : r + 1], 1.0, 0.0).astype(BF16)
                match = iota((256, 128), 0) == key2[r : r + 1]
                high, low = parts_of(weight[r : r + 1], 2)
                rhs[:256, cols] = jnp.where(match, high.astype(F32), 0.0).astype(BF16)
                rhs[256:, cols] = jnp.where(match, low.astype(F32), 0.0).astype(BF16)
            both = dot_nt(lhs[...], rhs[...])
            if a == 0 and q == 0:
                weights[...] = both[:, :256] + both[:, 256:]
            else:
                weights[...] += both[:, :256] + both[:, 256:]

    run_step(3)

    next_phase(2)

    run_step(4)

    for copy in shares:
        copy.wait_recv()
    combined4 = jnp.zeros((128, 256), F32)
    for q in range(4):
        block = table[q // 2, (q % 2) * 32 : (q % 2) * 32 + 32].reshape(256, 256)
        t_high, t_low = parts_of(block, 2)
        w_high, w_low = parts_of(weights[q * 128 : (q + 1) * 128, :], 2)
        combined4 += dot_nn(w_high, t_high) + dot_nn(w_high, t_low) + dot_nn(w_low, t_high)
    combined = combined4[:32, :64]
    for r in range(1, 4):
        combined += combined4[r * 32 : (r + 1) * 32, r * 64 : (r + 1) * 64]
    for r in range(4):
        ycol[r] = dot_tn(combined[r * 8 : r * 8 + 8].astype(BF16), in_block)

    def add_member(m, acc):
        rows = [jnp.broadcast_to(ycol[r, pl.ds(m, 1), :], (BLK, TLON)) for r in range(4)]
        return acc + ens[m].astype(F32) * jnp.concatenate(rows, axis=0)

    prior_ref[...] = lax.fori_loop(0, MEM, add_member, var_ref[...] * prior_ref[...])

    for copy in outs:
        copy.wait()
    flights = edges + courants + routes + routes2 + shares
    flights += [copy for group in gathers for copy in group]
    flights += [copy for group in sent.values() for copy in group]
    for copy in flights:
        copy.wait_send()


def per_device(ce, cn, cells, misfit, kern, ens, psrc, pdst, taper, var):
    vmem = pl.BlockSpec(memory_space=pltpu.VMEM)
    hbm = pl.BlockSpec(memory_space=pl.ANY)
    tile = (TLAT, TLON)
    return pl.pallas_call(
        kernel,
        out_shape=(
            jax.ShapeDtypeStruct((LEV,) + tile, F32),
            jax.ShapeDtypeStruct(tile, F32),
        ),
        in_specs=[hbm, hbm, vmem, vmem, pl.BlockSpec(memory_space=pltpu.SMEM), hbm, vmem, vmem, vmem, vmem],
        out_specs=(hbm, vmem),
        scratch_shapes=[
            pltpu.VMEM((LEV,) + tile, F32),
            pltpu.VMEM((LEV, TLAT + 8, TLON), F32),
            pltpu.VMEM((LEV,) + tile, F32),
            pltpu.VMEM((LEV,) + tile, F32),
            pltpu.VMEM((LEV,) + tile, F32),
            pltpu.VMEM((LEV, ROWS, TLON), F32),
            pltpu.VMEM((LEV,) + tile, F32),
            pltpu.VMEM((MEM,) + tile, BF16),
            pltpu.VMEM((EXT, ROWS, TLON), F32),
            pltpu.VMEM((ROWS, TLON), F32),
            pltpu.VMEM((ROWS, TLON), F32),
            pltpu.VMEM(tile, F32),
            pltpu.VMEM(tile, F32),
            pltpu.VMEM(tile, F32),
            pltpu.VMEM(tile, F32),
            pltpu.VMEM((LEV, TLON), F32),
            pltpu.VMEM((LEV, TLON), F32),
            pltpu.VMEM((5,) + tile, F32),
        ]
        + [pltpu.VMEM((ROUNDS, GROUPS) + tile, F32) for _ in range(4)]
        + [pltpu.VMEM((ROUNDS, GROUPS, KG, TLON), F32) for _ in range(4)]
        + [
            pltpu.VMEM((NLON, 2, 8, 128), F32),
            pltpu.VMEM((NLON, 2, 8, 128), F32),
            pltpu.VMEM((NLAT, 2, 16, 128), F32),
            pltpu.VMEM((NLAT, 2, 16, 128), F32),
            pltpu.VMEM((512, 1024), BF16),
            pltpu.VMEM((512, 1024), BF16),
            pltpu.VMEM((512, 256), F32),
            pltpu.VMEM((256 * 8, TLON), F32),
            pltpu.VMEM((8, 256), F32),
            pltpu.VMEM((2, 64, 8, 256), F32),
            pltpu.VMEM((4, MEM, TLON), F32),
            pltpu.SemaphoreType.DMA((3,)),
            pltpu.SemaphoreType.DMA((GROUPS,)),
            pltpu.SemaphoreType.DMA((COPIES,)),
            pltpu.SemaphoreType.DMA((COPIES,)),
        ],
        compiler_params=pltpu.CompilerParams(
            collective_id=0, has_side_effects=True, vmem_limit_bytes=48 * 1024 * 1024
        ),
    )(
        ce, cn, cells.reshape(8, 128), misfit.reshape(FIELDS, 8, 128), kern, ens,
        psrc.reshape(8, 128), pdst.reshape(8, 128), taper.reshape(8, 128), var,
    )


def solution(mesh):
    in_specs = (
        P(None, "lat", "lon"),
        P(None, "lat", "lon"),
        P("lat", "lon", None),
        P(None, "lat", "lon", None),
        P(),
        P(None, "lat", "lon"),
        P(("lon", "lat")),
        P(("lon", "lat")),
        P(("lon", "lat")),
        P("lat", "lon"),
    )
    out_specs = (P(None, "lat", "lon"), P("lat", "lon"))
    return jax.shard_map(
        per_device, mesh=mesh, in_specs=in_specs, out_specs=out_specs, check_vma=False
    )
```

time: 1200 us -> 94.5 us (0.08); the launches traced: 1180 us -> 93.8 us
  waiting for transfers between devices: 948 us -> 0 us
  other arithmetic: 98.3 us -> 0 us
  Pallas kernels: 0 us -> 83.4 us
  local copies, waits for them, and re-layouts: 71.3 us -> 9.79 us
  starting transfers between devices: 38.5 us -> 0 us
  between operations: 14.9 us -> 0.66 us
    reduce_scatter x1 -> x0, waiting for transfers between devices: 638 us -> none  [per_device(): lax.psum_scatter(partial_sums, ('lon', 'lat'), scatter_dimension=0, tiled...]
    all_gather x1 -> x0, waiting for transfers between devices: 305 us -> none  [per_device(): lax.all_gather(local_coeffs, ('lon', 'lat'), axis=0, tiled=True)]
    pallas_call x0 -> x1, Pallas kernels: none -> 83.4 us  [per_device(): pl.pallas_call(kernel, out_shape=(jax.ShapeDtypeStruct((LEV,) + tile, F32...]
    add x5 -> x0, other arithmetic: 45.1 us -> none  [the longest x4 44.5 us: per_device(): adj_field + pos_east * (east_vals - adj_field)]
    scatter-add x6 -> x0, other arithmetic: 44.4 us -> none  [the longest x5 30.5 us: forcing(): column = jnp.zeros((tile_lat * tile_lon,), jnp.float32).at[flat_cells].ad...]
    slice x20 -> x0, local copies, waits for them, and re-layouts: 40.6 us -> none  [the longest x12 23.6 us: with_halo(): lax.slice_in_dim(block, 0, width, axis=dim)]
    ppermute x18 -> x0, starting transfers between devices: 38.1 us -> none  [the longest x8 23.4 us: with_halo(): lax.ppermute(lax.slice_in_dim(block, 0, width, axis=dim), axis, backward)]
    ppermute x9 -> x0, local copies, waits for them, and re-layouts: 23.8 us -> none  [the longest x4 10.3 us: with_halo(): lax.ppermute(lax.slice_in_dim(block, 0, width, axis=dim), axis, backward)]
  transfers between devices with their start and end apart: 20 -> 0, of which waited for: 8 -> 0; matrix products, arithmetic and copies ran while one was open for 6% -> 0% of each run, Pallas kernels for 0% -> 0%
where the time goes in v1:
time: 94.5 us; the launch traced here: 93.8 us
  Pallas kernels  83.4 us (88%)
  local copies, waits for them, and re-layouts  9.79 us (10%)
    pallas_call x1, Pallas kernels, per_device(): pl.pallas_call(kernel, out_shape=(jax.ShapeDtypeStruct((LEV,) + tile, F32...  83.4 us
    unnamed x20, local copies, waits for them, and re-layouts  9.79 us

profile of v1, /device:TPU:1, one launch (start us, length us, event | category | flops | bytes accessed | tf_op | source)
XLA Modules:
  0.0 93.8 jit_solution(14082571526059804955)
XLA Ops:
  0.6 0.0 copy-start
  0.6 1.7 %copy-done = f32[72,64,128]{2,1,0:T(8,128)S(1)} copy-done((f32[72,64,128]{2,1,0:T(8,128)S(1)}, f32[72,64,128]{2,1,0:T(8,128)}, u32[]{:S(2)}) %copy-start) | copy-done | bytes 2359320
  2.3 0.0 copy-start.1
  2.3 1.2 %copy-done.1 = bf16[64,64,128]{2,1,0:T(8,128)(2,1)S(1)} copy-done((bf16[64,64,128]{2,1,0:T(8,128)(2,1)S(1)}, bf16[64,64,128]{2,1,0:T(8,128)(2,1)}, u32[]{:S(2)}) %copy-start.1) | copy-done | bytes 1048600
  3.5 0.0 copy-start.2
  3.5 0.8 copy-done.2
  4.3 0.0 copy-start.3
  4.3 0.7 copy-done.3
  5.0 0.0 copy-start.4
  5.0 0.7 copy-done.4
  5.7 0.0 copy-start.5
  5.7 0.7 copy-done.5
  6.4 0.0 copy-start.6
  6.4 0.7 copy-done.6
  7.1 0.0 copy-start.7
  7.1 0.7 copy-done.7
  7.8 0.0 copy-start.8
  7.8 0.7 copy-done.8
  8.4 83.4 %shard_map.113 = (f32[72,64,128]{2,1,0:T(8,128)S(1)}, f32[64,128]{1,0:T(8,128)S(1)}) custom-call(f32[72,64,128]{2,1,0:T(8,128)S(1)} %copy-done, f32[72,64,128]{2,1,0:T(8,128)} %cn_hbm.1, s32[8,128]{1,0:T(8,128)S(1)} %bitcast.6, f32[5,8,128]{2,1,0:T(8,128)S(1)} %bitcast.5, f32[72]{0:T(128)S(1)} %copy-done.8, bf16[64,64,128]{2,1,0:T(8,128)(2,1)S(1)} %copy-done.1, ...), custom_call_target="tpu_custom_call" | custom-call | tf_op jit(solution)/shard_map/pallas_call | solution.py:462
  91.8 1.4 %copy.14 = f32[72,64,128]{2,1,0:T(8,128)} copy(f32[72,64,128]{2,1,0:T(8,128)S(1)} %get-tuple-element.4) | data formatting | bytes 4718592
  93.2 0.6 copy.15
Async XLA Ops:
  0.6 1.7 %copy-start = (f32[72,64,128]{2,1,0:T(8,128)S(1)}, f32[72,64,128]{2,1,0:T(8,128)}, u32[]{:S(2)}) copy-start(f32[72,64,128]{2,1,0:T(8,128)} %ce_hbm.1) | copy-start | bytes 7077892
  2.3 1.2 %copy-start.1 = (bf16[64,64,128]{2,1,0:T(8,128)(2,1)S(1)}, bf16[64,64,128]{2,1,0:T(8,128)(2,1)}, u32[]{:S(2)}) copy-start(bf16[64,64,128]{2,1,0:T(8,128)(2,1)} %ens_hbm.1) | copy-start | bytes 3145732
  3.5 0.8 copy-start.2
  4.3 0.7 copy-start.3
  5.0 0.7 copy-start.4
  5.7 0.7 copy-start.5
  6.4 0.7 copy-start.6
  7.1 0.7 copy-start.7
  7.8 0.7 copy-start.8

commit v2 on v1

v2 whole, which is shorter than its diff:
```python
import functools

import jax
import jax.numpy as jnp
from jax import lax
from jax.experimental import pallas as pl
from jax.experimental.pallas import tpu as pltpu
from jax.sharding import PartitionSpec as P

MESH = pl.DeviceIdType.MESH
F32, BF16, I32, I16 = jnp.float32, jnp.bfloat16, jnp.int32, jnp.int16

TLAT, TLON, LEV, BLK, MEM = 64, 128, 72, 16, 64
NLON, NLAT = 16, 8
FIELDS = 5
EXT = 7
ROWS = TLAT + 16
GROUPS = 3
PIECES = 8
KG = LEV // GROUPS
LEVELS = 24
ROUNDS = 3
CHUNKS = 8
COPIES = 8 + 2 + 4 * ROUNDS * GROUPS + 15 + 7 + 1 + 9 + 9


def iota(shape, dim):
    return lax.broadcasted_iota(I32, shape, dim)


def dot_nt(a, b):
    return lax.dot_general(a, b, (((1,), (1,)), ((), ())), preferred_element_type=F32)


def dot_tn(a, b):
    return lax.dot_general(a, b, (((0,), (0,)), ((), ())), preferred_element_type=F32)


def dot_nn(a, b):
    return lax.dot_general(a, b, (((1,), (0,)), ((), ())), preferred_element_type=F32)


def spread_row(row, dtype, rows):
    few = jnp.broadcast_to(row, (16, 128)).astype(dtype)
    return jnp.concatenate([few] * (rows // 16), axis=0)


def select(mask, row, rows):
    return jnp.where(mask, spread_row(row, BF16, rows), jnp.zeros((), BF16))


def one_hot(mask):
    return jnp.where(mask, jnp.ones((), BF16), jnp.zeros((), BF16))


def parts_of(x, count):
    parts = []
    for _ in range(count):
        part = x.astype(BF16)
        parts.append(part)
        x = x - part.astype(F32)
    return parts


def kernel(
    ce_hbm, cn_hbm, cells_hbm, misfit_hbm, kern_hbm, ens_hbm, psrc_hbm, pdst_hbm, taper_hbm, var_hbm,
    out_hbm, prior_hbm,
    cells, misfit, kern, psrc, pdst, taper, var_ref,
    ce, cn, aw, asn, c0, field, field16, last, ens, area, halo_e, halo_w, pack_e, pack_w,
    cpack, chalo, crow, crhalo, shifted,
    fpack, fhalo_e, fhalo_w, move, ends, every, to_first, frow_n, frow_s, frhalo_n, frhalo_s,
    slots1, route1, slots2, route2, keys, weights, weights16,
    partial, own, table, ycol, prior,
    local_sem, out_sem, send_sem, recv_sem,
):
    lon, lat = lax.axis_index("lon"), lax.axis_index("lat")
    core, x, y_lo = lon % 2, (lon // 2) % 4, lon // 8
    z, y_hi = lat // 2, lat % 2
    y = y_hi * 2 + y_lo

    def shift_lon(s):
        return (lon + s + NLON) % NLON

    def shift_lat(s):
        return (lat + s + NLAT) % NLAT

    def device(xx, yy, zz, cc):
        return {"lon": (yy % 2) * 8 + xx * 2 + cc, "lat": zz * 2 + yy // 2}

    rest = pl.ds(1, LEV - 1)
    ce_in = pltpu.make_async_copy(ce_hbm.at[rest], ce.at[rest], local_sem.at[0])
    cn_in = pltpu.make_async_copy(cn_hbm.at[rest], cn.at[rest, pl.ds(8, TLAT), :], local_sem.at[1])
    ens_in = pltpu.make_async_copy(ens_hbm, ens, local_sem.at[2])
    small = [
        pltpu.make_async_copy(src, dst, local_sem.at[3 + n])
        for n, (src, dst) in enumerate((
            (cells_hbm, cells), (misfit_hbm, misfit), (kern_hbm, kern), (psrc_hbm, psrc),
            (pdst_hbm, pdst), (taper_hbm, taper), (var_hbm, var_ref),
            (ce_hbm.at[0], ce.at[0]), (cn_hbm.at[0], cn.at[0, pl.ds(8, TLAT), :]),
        ))
    ]
    for copy in small + [ce_in, cn_in, ens_in]:
        copy.start()

    barrier = pltpu.get_barrier_semaphore()
    peers = [{"lon": shift_lon(i), "lat": lat} for i in range(1, NLON)]
    peers += [{"lon": lon, "lat": shift_lat(i)} for i in range(1, NLAT)]
    peers += [device(x, (y + i) % 4, z, core) for i in (1, 3)]
    peers += [{"lon": shift_lon(i), "lat": shift_lat(j)} for i in (-1, 1) for j in (-1, 1)]
    for peer in peers:
        pl.semaphore_signal(barrier, inc=1, device_id=peer, device_id_type=MESH)

    used = [0]

    def remote(src, dst, peer):
        n = used[0]
        used[0] += 1
        return pltpu.make_async_remote_copy(
            src_ref=src, dst_ref=dst, send_sem=send_sem.at[n], recv_sem=recv_sem.at[n],
            device_id=peer, device_id_type=MESH,
        )

    lane = iota((TLAT, TLON), 1)
    lane32 = lane % 32

    row, col = iota((256, 256), 0), iota((256, 256), 1)
    shift = (row < 128) & (((col < 128) & (row == col + 1)) | ((col >= 128) & (row + 129 == col)))
    edge = ((row >= 160) & (row < 192) & (col == 127)) | ((row >= 128) & (row < 160) & (col == 128))
    move[...] = jnp.where(shift | edge, 1.0, 0.0).astype(BF16)
    end = ((row % 128 == 127) & (col % 128 < 32)) | ((row % 128 == 0) & (col % 128 >= 32) & (col % 128 < 64))
    end = end & (row // 128 == col // 128)
    ends[...] = jnp.where(end, 1.0, 0.0).astype(BF16)
    row, col = iota((128, 128), 0), iota((128, 128), 1)
    every[...] = jnp.where(row == 127, 1.0, 0.0).astype(BF16)
    to_first[...] = jnp.where(col == 0, 1.0, 0.0).astype(BF16)

    for copy in small:
        copy.wait()

    columns = [jnp.zeros((TLAT, TLON), F32) for _ in range(FIELDS)]
    cell_row, cell_col = cells[...] >> 7, cells[...] & 127
    number = iota((128, 128), 0).astype(I16)
    for q in range(CHUNKS):
        in_row = number[:TLAT] == spread_row(cell_row[q : q + 1], I16, TLAT)
        in_col = one_hot(number == spread_row(cell_col[q : q + 1], I16, TLON))
        weighted = []
        for t in range(FIELDS):
            for part in parts_of(misfit[t, q : q + 1, :], 2):
                weighted.append(select(in_row, part.astype(F32), TLAT))
        placed = dot_nt(jnp.concatenate(weighted, axis=0), in_col)
        for t in range(FIELDS):
            base = 2 * t * TLAT
            columns[t] += placed[base : base + TLAT] + placed[base + TLAT : base + 2 * TLAT]
    for t in range(FIELDS):
        area[t, 8 : 8 + TLAT, :] = columns[t]

    area[5, 8 : 8 + TLAT, :] = ce[0]
    area[6, 8 : 8 + TLAT, :] = cn[0, 8 : 8 + TLAT, :]
    first = jnp.zeros((TLAT, TLON), F32)
    final = jnp.zeros((TLAT, TLON), F32)
    for n in range(EXT):
        value = area[n, 8 : 8 + TLAT, :]
        here = (lane >= 4 * n) & (lane < 4 * n + 4)
        first = jnp.where(here, pltpu.roll(value, 4 * n, 1) if n else value, first)
        final = jnp.where(here, pltpu.roll(value, 4 * n + 4, 1), final)
    pack_w[...] = first
    pack_e[...] = final

    pl.semaphore_wait(barrier, len(peers))

    east = {"lon": shift_lon(1), "lat": lat}
    west = {"lon": shift_lon(-1), "lat": lat}
    north = {"lon": lon, "lat": shift_lat(1)}
    south = {"lon": lon, "lat": shift_lat(-1)}
    mid, low8, high8 = pl.ds(8, TLAT), pl.ds(0, 8), pl.ds(TLAT + 8, 8)
    edges = [
        remote(area.at[:, pl.ds(TLAT, 8), :], area.at[:, low8, :], north),
        remote(area.at[:, pl.ds(8, 8), :], area.at[:, high8, :], south),
        remote(pack_e.at[pl.ds(TLAT - 8, 8), :], halo_w.at[low8, :], {"lon": shift_lon(1), "lat": shift_lat(1)}),
        remote(pack_e.at[pl.ds(0, 8), :], halo_w.at[high8, :], {"lon": shift_lon(1), "lat": shift_lat(-1)}),
        remote(pack_w.at[pl.ds(TLAT - 8, 8), :], halo_e.at[low8, :], {"lon": shift_lon(-1), "lat": shift_lat(1)}),
        remote(pack_w.at[pl.ds(0, 8), :], halo_e.at[high8, :], {"lon": shift_lon(-1), "lat": shift_lat(-1)}),
        remote(pack_e, halo_w.at[mid, :], east),
        remote(pack_w, halo_e.at[mid, :], west),
    ]
    for copy in edges:
        copy.start()

    ce_in.wait()

    def pack_courant(kb, acc):
        faces = [ce[kb * 8 + i].astype(BF16) for i in range(8)]
        tips = dot_nn(jnp.concatenate(faces, axis=0), every[...])
        for i in range(8):
            acc = jnp.where(lane == kb * 8 + i, tips[i * TLAT : (i + 1) * TLAT], acc)
        return acc

    cpack[...] = lax.fori_loop(0, LEV // 8, pack_courant, jnp.zeros((TLAT, TLON), F32))
    cn_in.wait()
    cn_rows = cn.reshape(LEV * (TLAT + 8), TLON)
    last_row = cn_rows[pl.ds(TLAT + 7, LEV, stride=TLAT + 8), :] * jnp.where(lat < NLAT - 1, 1.0, 0.0)
    crow[...] = last_row
    cn_rows[pl.ds(TLAT + 7, LEV, stride=TLAT + 8), :] = last_row
    courants = [remote(crow, crhalo, north), remote(cpack, chalo, east)]
    for copy in courants:
        copy.start()

    total = jnp.zeros((128, 128), F32)
    slot1 = jnp.zeros((128, 128), F32)
    slot2 = jnp.zeros((128, 128), F32)
    before = jnp.where(iota((128, 128), 0) < iota((128, 128), 1), 1.0, 0.0).astype(BF16)
    ones = jnp.ones((128, 128), BF16)
    src, dst = psrc[...], pdst[...]
    s_lon, s_lat = src >> 8, (src >> 5) & 7
    s_x, s_y, s_z = (s_lon >> 1) & 3, (s_lat & 1) * 2 + (s_lon >> 3), s_lat >> 1
    s_slot = jnp.where((s_lon & 1) == 0, s_z * 16 + s_y * 4 + s_x, s_x * 16 + s_z * 4 + s_y)
    key1 = ((s_lon & 1) * 128 + ((src >> 3) & 3) * 32 + (dst & 31)).astype(F32)
    key2_high, key2_low = (s_slot * 8).astype(F32), (src & 7).astype(F32)
    tile = dst >> 5
    for q in range(CHUNKS):
        at = slice(q, q + 1)
        here = iota((128, 128), 0) == tile[at]
        mine = number == spread_row(tile[at], I16, 128)
        mark = one_hot(mine)
        count = dot_nn(mark, before) + total
        total += dot_nn(mark, ones)
        rank = jnp.sum(jnp.where(here, count, 0.0), axis=0, keepdims=True).astype(I32)
        at_low = one_hot(number == spread_row(rank, I16, 128))
        at_high = one_hot(number == spread_row(rank + 64, I16, 128))
        slot1 += dot_nt(select(mine, key1[at], 128), at_low)
        slot1 += dot_nt(select(mine, key2_high[at], 128), at_high)
        slot1 += dot_nt(select(mine, key2_low[at], 128), at_high)
        slot2 += dot_nt(select(mine, taper[at, :], 128), at_low)
    for d in range(NLON):
        slots1[d, 0] = slot1[d * 8 : d * 8 + 8]
        slots1[d, 1] = slot2[d * 8 : d * 8 + 8]

    routes = [
        remote(slots1.at[shift_lon(i)], route1.at[lon], {"lon": shift_lon(i), "lat": lat})
        for i in range(1, NLON)
    ]
    for copy in routes:
        copy.start()

    for copy in edges:
        copy.wait_recv()

    wide_lane = iota((ROWS, TLON), 1)

    def widened(n):
        from_east = halo_e[...] if n == 0 else pltpu.roll(halo_e[...], 128 - 4 * n, 1)
        from_west = pltpu.roll(halo_w[...], 124 - 4 * n, 1)
        side = jnp.where(wide_lane < 64, from_east, from_west)
        return jnp.concatenate([area[n], side], axis=1)

    def up(v, axis):
        return pltpu.roll(v, v.shape[axis] - 1, axis)

    def down(v, axis):
        return pltpu.roll(v, 1, axis)

    forced = [widened(t) for t in range(FIELDS)]
    east0 = widened(5)
    global_row = lat * TLAT - 8 + iota((ROWS, 2 * TLON), 0)
    inside = (global_row >= 0) & (global_row < NLAT * TLAT - 1)
    north0 = jnp.where(inside, widened(6), 0.0)
    pe0, pn0 = jnp.maximum(east0, 0.0), jnp.maximum(north0, 0.0)
    aw0, as0 = -jnp.minimum(down(east0, 1), 0.0), -jnp.minimum(down(north0, 0), 0.0)
    c00 = 1.0 - pe0 - aw0 - pn0 - as0
    k0 = kern[0]
    level = k0 * forced[0]
    surface_wide = level
    for t in range(1, FIELDS):
        level = (
            c00 * level + pe0 * up(level, 1) + aw0 * down(level, 1)
            + pn0 * up(level, 0) + as0 * down(level, 0) + k0 * forced[t]
        )
        surface_wide = surface_wide + level
    surface = surface_wide[8 : 8 + TLAT, :TLON]
    prior[...] = surface
    base = forced[0]
    for n, v in enumerate((base, up(base, 1), down(base, 1), up(base, 0), down(base, 0))):
        shifted[n] = v[8 : 8 + TLAT, :TLON]

    ens_in.wait()
    rounded = surface.astype(BF16).astype(F32)

    @pl.loop(0, MEM)
    def _(m):
        product = ens[m].astype(F32) * rounded
        for r in range(4):
            at = pl.multiple_of((r * MEM + m) * 8, 8)
            partial[pl.ds(at, 8), :] = product[r * 16 : r * 16 + 8] + product[r * 16 + 8 : r * 16 + 16]

    row_sums = partial[pl.ds(0, 256, stride=8), :]
    for s in range(1, 8):
        row_sums += partial[pl.ds(s, 256, stride=8), :]
    in_block = jnp.where(iota((8, TLON), 0) == iota((8, TLON), 1) // BLK, 1.0, 0.0).astype(BF16)
    own[...] = sum(dot_nt(in_block, part) for part in parts_of(row_sums, 3))

    slot = jnp.where(core == 0, z * 16 + y * 4 + x, x * 16 + z * 4 + y)
    sibling = device(x, y, z, 1 - core)
    moves = [(1 - core, core, 0), (0, 1 - core, core), (core, 0, 1 - core)]

    def ring_peer(phase, s):
        dx, dy, dz = moves[phase]
        return device((x + s * dx) % 4, (y + s * dy) % 4, (z + s * dz) % 4, core)

    def gather_sends(phase):
        if phase == 0:
            src, dst = own, table.at[core, slot]
        else:
            size = 4**phase
            first_slot = slot // size * size
            src = table.at[core, pl.ds(first_slot, size)]
            dst = table.at[core, pl.ds(first_slot, size)]
        return [remote(src, dst, ring_peer(phase, s)) for s in (2, 1, 3)]

    def share_sends(phase):
        size = 4**phase
        group = slot // (4 * size) * (4 * size)
        place = slot // size % 4
        copies = []
        for s in (1, 3, 2):
            rows = pl.ds(group + (place + s) % 4 * size, size)
            copies.append(remote(table.at[core, rows], table.at[core, rows], sibling))
        return copies

    shares = [remote(own, table.at[core, slot], sibling)]
    gathers = [gather_sends(0)]
    for copy in gathers[0] + shares:
        copy.start()
    table[core, slot] = own[...]

    def next_phase(phase):
        for copy in gathers[phase]:
            copy.wait_recv()
        if phase < 2:
            gathers.append(gather_sends(phase + 1))
            for copy in gathers[phase + 1]:
                copy.start()
        more = share_sends(phase)
        for copy in more:
            copy.start()
        shares.extend(more)

    for copy in courants:
        copy.wait_recv()
    cn_rows[pl.ds(7, LEV, stride=TLAT + 8), :] = crhalo[...] * jnp.where(lat > 0, 1.0, 0.0)
    field_rows = field.reshape(LEV * ROWS, TLON)

    def block(t, g, halo, kb, pack):
        base = g * KG + kb * LEVELS
        if t > 1:
            rows = []
            for i in range(LEVELS):
                mine = jnp.where(lane32 == kb * LEVELS + i, halo, 0.0).astype(BF16)
                rows.append(jnp.concatenate([field16[base + i], mine], axis=1))
            moved = dot_nn(jnp.concatenate(rows, axis=0), move[...])
        else:
            rows = [jnp.where(lane == base + i, halo, 0.0).astype(BF16) for i in range(LEVELS)]
            moved = dot_nn(jnp.concatenate(rows, axis=0), to_first[...])
        rounded = []
        for i in range(LEVELS):
            k = base + i
            kk = kern[k]
            if t == 1:
                faces = ce[k]
                pe = jnp.maximum(faces, 0.0)
                behind = jnp.where(lane == 0, moved[i * TLAT : (i + 1) * TLAT], pltpu.roll(faces, 1, 1))
                w = jnp.minimum(behind, 0.0)
                pn = jnp.maximum(cn[k, 8 : 8 + TLAT, :], 0.0)
                s = jnp.minimum(cn[k, 7 : 7 + TLAT, :], 0.0)
                c = (1.0 - pe) + w - pn + s
                ce[k] = pe
                cn[k, 8 : 8 + TLAT, :] = pn
                aw[k], asn[k], c0[k] = w, s, c
                new = kk * (
                    c * shifted[0] + pe * shifted[1] - w * shifted[2] + pn * shifted[3] - s * shifted[4]
                    + area[1, 8 : 8 + TLAT, :]
                )
            else:
                level_rows = slice(i * TLAT, (i + 1) * TLAT)
                new = (
                    c0[k] * field[k, 8 : 8 + TLAT, :]
                    + ce[k] * moved[level_rows, :TLON] - aw[k] * moved[level_rows, TLON:]
                    + cn[k, 8 : 8 + TLAT, :] * field[k, 9 : 9 + TLAT, :]
                    - asn[k] * field[k, 7 : 7 + TLAT, :] + kk * area[t, 8 : 8 + TLAT, :]
                )
            if t == 4:
                last[k] = new
                continue
            field[k, 8 : 8 + TLAT, :] = new
            new16 = new.astype(BF16)
            field16[k] = new16
            rounded.append(new16)
        if t == 4:
            return pack
        pairs = [jnp.concatenate(rounded[i : i + 2], axis=1) for i in range(0, LEVELS, 2)]
        tips = dot_nn(jnp.concatenate(pairs, axis=0), ends[...])
        for i in range(LEVELS):
            tip = tips[i // 2 * TLAT : (i // 2 + 1) * TLAT, i % 2 * TLON : (i % 2 + 1) * TLON]
            pack = jnp.where(lane32 == kb * LEVELS + i, tip, pack)
        return pack

    sent = {}
    outs = []

    def run_group(t, g):
        start = g * KG * ROWS
        halo = chalo[...]
        if t > 1:
            for copy in sent[t - 1, g]:
                copy.wait_recv()
            field_rows[pl.ds(start + 7, KG, stride=ROWS), :] = frhalo_s[t - 2, g]
            field_rows[pl.ds(start + 8 + TLAT, KG, stride=ROWS), :] = frhalo_n[t - 2, g]
            halo = jnp.where(lane < 32, fhalo_w[t - 2, g], fhalo_e[t - 2, g])
        run = functools.partial(block, t, g, halo)
        pack = lax.fori_loop(0, KG // LEVELS, run, 0 if t == 4 else jnp.zeros((TLAT, TLON), F32))
        if t == 4:
            levels = pl.ds(g * KG, KG)
            outs.append(pltpu.make_async_copy(last.at[levels], out_hbm.at[levels], out_sem.at[g]))
            outs[-1].start()
            return
        fpack[t - 1, g] = pack
        frow_n[t - 1, g] = field_rows[pl.ds(start + 7 + TLAT, KG, stride=ROWS), :]
        frow_s[t - 1, g] = field_rows[pl.ds(start + 8, KG, stride=ROWS), :]
        sent[t, g] = [
            remote(frow_n.at[t - 1, g], frhalo_s.at[t - 1, g], north),
            remote(frow_s.at[t - 1, g], frhalo_n.at[t - 1, g], south),
            remote(fpack.at[t - 1, g], fhalo_w.at[t - 1, g], east),
            remote(fpack.at[t - 1, g], fhalo_e.at[t - 1, g], west),
        ]
        for copy in sent[t, g]:
            copy.start()

    run_group(1, 0)

    route1[lon] = slots1[lon]
    for copy in routes:
        copy.wait_recv()
    for n in range(2):
        for a in range(NLAT):
            slots2[a, n] = jnp.concatenate([route1[d, n, a : a + 1, :] for d in range(NLON)], axis=0)
    routes2 = [
        remote(slots2.at[shift_lat(i)], route2.at[lat], {"lon": lon, "lat": shift_lat(i)})
        for i in range(1, NLAT)
    ]
    for copy in routes2:
        copy.start()
    route2[lat] = slots2[lat]

    run_group(1, 1)
    next_phase(0)
    run_group(1, 2)

    run_group(2, 0)
    run_group(2, 1)
    next_phase(1)
    run_group(2, 2)

    for copy in routes2:
        copy.wait_recv()
    half = iota((16, 128), 1) < 64
    for a in range(4):
        one, two = route2[a, 0], route2[a + 4, 0]
        at = slice(a * 16, a * 16 + 16)
        keys[0, at] = jnp.where(half, one, pltpu.roll(two, 64, 1))
        keys[1, at] = jnp.where(half, pltpu.roll(one, 64, 1), two)
        keys[2, at] = jnp.where(half, route2[a, 1], pltpu.roll(route2[a + 4, 1], 64, 1))
    weights[...] = jnp.zeros_like(weights)

    def add_weights(i, carry):
        at = pl.ds(pl.multiple_of(i * 8, 8), 8)
        key1, key2, weight = keys[0, at, :].astype(I32), keys[1, at, :].astype(I32), keys[2, at, :]
        number = iota((128, 128), 0).astype(I16)
        lhs, rhs = [], []
        for u in range(8):
            one = slice(u, u + 1)
            match = [number == spread_row(key1[one] - r, I16, 128) for r in (0, 128)]
            lhs.append(jnp.concatenate([select(m, weight[one], 128) for m in match], axis=0))
            match = [number == spread_row(key2[one] - r, I16, 128) for r in (0, 128, 256, 384)]
            rhs.append(jnp.concatenate([one_hot(m) for m in match], axis=0))
        weights[...] += dot_nt(jnp.concatenate(lhs, axis=1), jnp.concatenate(rhs, axis=1))
        return carry

    lax.fori_loop(0, 4, add_weights, 0)

    run_group(3, 0)
    run_group(3, 1)
    next_phase(2)
    run_group(3, 2)

    lax.fori_loop(4, 8, add_weights, 0)
    w_parts = parts_of(weights[...], 2)
    weights16[0] = w_parts[0]
    weights16[1] = w_parts[1]

    run_group(4, 0)

    for copy in shares:
        copy.wait_recv()
    combined4 = jnp.zeros((128, 256), F32)
    for q in range(4):
        table_part = table[q // 2, (q % 2) * 32 : (q % 2) * 32 + 32].reshape(256, 256)
        t_high, t_low = parts_of(table_part, 2)
        w_rows, w_cols = slice(q // 2 * 128, q // 2 * 128 + 128), slice(q % 2 * 256, q % 2 * 256 + 256)
        w_high, w_low = weights16[0, w_rows, w_cols], weights16[1, w_rows, w_cols]
        combined4 += dot_nn(w_high, t_high) + dot_nn(w_high, t_low) + dot_nn(w_low, t_high)
    combined = combined4[:32, :64]
    for r in range(1, 4):
        combined += combined4[r * 32 : (r + 1) * 32, r * 64 : (r + 1) * 64]
    for r in range(4):
        ycol[r] = dot_tn(combined[r * 8 : r * 8 + 8].astype(BF16), in_block)

    def add_member(m, acc):
        rows = [jnp.broadcast_to(ycol[r, pl.ds(m, 1), :], (BLK, TLON)) for r in range(4)]
        return acc + ens[m].astype(F32) * jnp.concatenate(rows, axis=0)

    prior[...] = lax.fori_loop(0, MEM, add_member, var_ref[...] * prior[...], unroll=8)
    outs.append(pltpu.make_async_copy(prior, prior_hbm, out_sem.at[GROUPS]))
    outs[-1].start()

    run_group(4, 1)
    run_group(4, 2)

    for copy in outs:
        copy.wait()
    flights = edges + courants + routes + routes2 + shares
    flights += [copy for group in gathers for copy in group]
    flights += [copy for group in sent.values() for copy in group]
    for copy in flights:
        copy.wait_send()


def hand_over(field, prior, field_out, prior_out, field_held, prior_held, in_sem, out_sem):
    steps = LEV // PIECES
    parts = [(prior, prior_held, prior_out)]
    for n in range(PIECES):
        levels = pl.ds(n * steps, steps)
        parts.append((field.at[levels], field_held.at[levels], field_out.at[levels]))
    loads = [
        pltpu.make_async_copy(src, held, in_sem.at[n]) for n, (src, held, _) in enumerate(parts)
    ]
    stores = [
        pltpu.make_async_copy(held, dst, out_sem.at[n]) for n, (_, held, dst) in enumerate(parts)
    ]
    for load in loads:
        load.start()
    for load, store in zip(loads, stores):
        load.wait()
        store.start()
    for store in stores:
        store.wait()


def per_device(ce, cn, cells, misfit, kern, ens, psrc, pdst, taper, var):
    hbm = pl.BlockSpec(memory_space=pl.ANY)
    tile = (TLAT, TLON)
    field, prior = pl.pallas_call(
        kernel,
        out_shape=(
            jax.ShapeDtypeStruct((LEV,) + tile, F32),
            jax.ShapeDtypeStruct(tile, F32),
        ),
        in_specs=[hbm] * 10,
        out_specs=(hbm, hbm),
        scratch_shapes=[
            pltpu.VMEM((8, 128), I32),
            pltpu.VMEM((FIELDS, 8, 128), F32),
            pltpu.SMEM((LEV,), F32),
            pltpu.VMEM((8, 128), I32),
            pltpu.VMEM((8, 128), I32),
            pltpu.VMEM((8, 128), F32),
            pltpu.VMEM(tile, F32),
            pltpu.VMEM((LEV,) + tile, F32),
            pltpu.VMEM((LEV, TLAT + 8, TLON), F32),
            pltpu.VMEM((LEV,) + tile, F32),
            pltpu.VMEM((LEV,) + tile, F32),
            pltpu.VMEM((LEV,) + tile, F32),
            pltpu.VMEM((LEV, ROWS, TLON), F32),
            pltpu.VMEM((LEV,) + tile, BF16),
            pltpu.VMEM((LEV,) + tile, F32),
            pltpu.VMEM((MEM,) + tile, BF16),
            pltpu.VMEM((EXT, ROWS, TLON), F32),
            pltpu.VMEM((ROWS, TLON), F32),
            pltpu.VMEM((ROWS, TLON), F32),
            pltpu.VMEM(tile, F32),
            pltpu.VMEM(tile, F32),
            pltpu.VMEM(tile, F32),
            pltpu.VMEM(tile, F32),
            pltpu.VMEM((LEV, TLON), F32),
            pltpu.VMEM((LEV, TLON), F32),
            pltpu.VMEM((5,) + tile, F32),
        ]
        + [pltpu.VMEM((ROUNDS, GROUPS) + tile, F32) for _ in range(3)]
        + [pltpu.VMEM((256, 256), BF16) for _ in range(2)]
        + [pltpu.VMEM((128, 128), BF16) for _ in range(2)]
        + [pltpu.VMEM((ROUNDS, GROUPS, KG, TLON), F32) for _ in range(4)]
        + [
            pltpu.VMEM((NLON, 2, 8, 128), F32),
            pltpu.VMEM((NLON, 2, 8, 128), F32),
            pltpu.VMEM((NLAT, 2, 16, 128), F32),
            pltpu.VMEM((NLAT, 2, 16, 128), F32),
            pltpu.VMEM((3, 64, 128), F32),
            pltpu.VMEM((256, 512), F32),
            pltpu.VMEM((2, 256, 512), BF16),
            pltpu.VMEM((256 * 8, TLON), F32),
            pltpu.VMEM((8, 256), F32),
            pltpu.VMEM((2, 64, 8, 256), F32),
            pltpu.VMEM((4, MEM, TLON), F32),
            pltpu.VMEM(tile, F32),
            pltpu.SemaphoreType.DMA((12,)),
            pltpu.SemaphoreType.DMA((GROUPS + 1,)),
            pltpu.SemaphoreType.DMA((COPIES,)),
            pltpu.SemaphoreType.DMA((COPIES,)),
        ],
        compiler_params=pltpu.CompilerParams(
            collective_id=0, has_side_effects=True, vmem_limit_bytes=60 * 1024 * 1024
        ),
    )(
        ce, cn, cells.reshape(8, 128), misfit.reshape(FIELDS, 8, 128), kern, ens,
        psrc.reshape(8, 128), pdst.reshape(8, 128), taper.reshape(8, 128), var,
    )
    return pl.pallas_call(
        hand_over,
        out_shape=(
            jax.ShapeDtypeStruct((LEV,) + tile, F32),
            jax.ShapeDtypeStruct(tile, F32),
        ),
        in_specs=[hbm] * 2,
        out_specs=(hbm, hbm),
        scratch_shapes=[
            pltpu.VMEM((LEV,) + tile, F32),
            pltpu.VMEM(tile, F32),
            pltpu.SemaphoreType.DMA((PIECES + 1,)),
            pltpu.SemaphoreType.DMA((PIECES + 1,)),
        ],
        compiler_params=pltpu.CompilerParams(vmem_limit_bytes=60 * 1024 * 1024),
    )(field, prior)


def solution(mesh):
    in_specs = (
        P(None, "lat", "lon"),
        P(None, "lat", "lon"),
        P("lat", "lon", None),
        P(None, "lat", "lon", None),
        P(),
        P(None, "lat", "lon"),
        P(("lon", "lat")),
        P(("lon", "lat")),
        P(("lon", "lat")),
        P("lat", "lon"),
    )
    out_specs = (P(None, "lat", "lon"), P("lat", "lon"))
    return jax.shard_map(
        per_device, mesh=mesh, in_specs=in_specs, out_specs=out_specs, check_vma=False
    )
```

time: 94.5 us -> 42.5 us (0.45)
  the two profiles are of different devices: /device:TPU:1 before, /device:TPU:0 now
where the time goes in v2:
time: 42.5 us; the launch traced here: 42.3 us
  Pallas kernels  41.7 us (98%)
  between operations  0.64 us (2%)
    pallas_call x1, Pallas kernels, per_device(): pl.pallas_call(kernel, out_shape=(jax.ShapeDtypeStruct((LEV,) + tile, F32...  39.2 us
    pallas_call x1, Pallas kernels, per_device(): pl.pallas_call(hand_over, out_shape=(jax.ShapeDtypeStruct((LEV,) + tile,...  2.53 us

profile of v2, /device:TPU:0, one launch (start us, length us, event | category | flops | bytes accessed | tf_op | source)
XLA Modules:
  0.0 42.3 jit_solution(6163841477742914750)
XLA Ops:
  0.6 39.2 %shard_map.113 = (f32[72,64,128]{2,1,0:T(8,128)}, f32[64,128]{1,0:T(8,128)}) custom-call(f32[72,64,128]{2,1,0:T(8,128)} %ce_hbm.1, f32[72,64,128]{2,1,0:T(8,128)} %cn_hbm.1, s32[8,128]{1,0:T(8,128)} %bitcast.6, f32[5,8,128]{2,1,0:T(8,128)} %bitcast.5, f32[72]{0:T(128)} %kern_hbm.1, bf16[64,64,128]{2,1,0:T(8,128)(2,1)} %ens_hbm.1, s32[8,128]{1,0:T(8,128)} %bitcast.7, ...), custom_call_target="tpu_custom_call" | custom-call | tf_op jit(solution)/shard_map/pallas_call | solution.py:560
  39.8 2.5 %shard_map.114 = (f32[72,64,128]{2,1,0:T(8,128)}, f32[64,128]{1,0:T(8,128)}) custom-call(f32[72,64,128]{2,1,0:T(8,128)} %get-tuple-element.4.field, f32[64,128]{1,0:T(8,128)} %get-tuple-element.5.prior), custom_call_target="tpu_custom_call" | custom-call | tf_op jit(solution)/shard_map/pallas_call | solution.py:625

commit v3 on v2

--- a/solution.py
+++ b/solution.py
@@ -1,5 +1,3 @@
-import functools
-
 import jax
 import jax.numpy as jnp
 from jax import lax
@@ -18,10 +16,10 @@
 GROUPS = 3
 PIECES = 8
 KG = LEV // GROUPS
-LEVELS = 24
+LEVELS = KG
 ROUNDS = 3
 CHUNKS = 8
-COPIES = 8 + 2 + 4 * ROUNDS * GROUPS + 15 + 7 + 1 + 9 + 9
+COPIES = 8 + 2 + 4 * ROUNDS * GROUPS + 15 + 7 + 15 + 1 + 3 + 3
 
 
 def iota(shape, dim):
@@ -88,6 +86,15 @@
         return {"lon": (yy % 2) * 8 + xx * 2 + cc, "lat": zz * 2 + yy // 2}
 
     rest = pl.ds(1, LEV - 1)
+    first_axis, second_axis, third_axis = (1 - core, core, 0), (0, 1 - core, core), (core, 0, 1 - core)
+
+    def plane_peer(i, j):
+        place = [(v + i * a + j * b) % 4 for v, a, b in zip((x, y, z), first_axis, second_axis)]
+        return device(*place, core)
+
+    def line_peer(i):
+        return device(*[(v + i * a) % 4 for v, a in zip((x, y, z), third_axis)], core)
+
     ce_in = pltpu.make_async_copy(ce_hbm.at[rest], ce.at[rest], local_sem.at[0])
     cn_in = pltpu.make_async_copy(cn_hbm.at[rest], cn.at[rest, pl.ds(8, TLAT), :], local_sem.at[1])
     ens_in = pltpu.make_async_copy(ens_hbm, ens, local_sem.at[2])
@@ -99,13 +106,13 @@
             (ce_hbm.at[0], ce.at[0]), (cn_hbm.at[0], cn.at[0, pl.ds(8, TLAT), :]),
         ))
     ]
-    for copy in small + [ce_in, cn_in, ens_in]:
+    for copy in small + [ce_in]:
         copy.start()
 
     barrier = pltpu.get_barrier_semaphore()
     peers = [{"lon": shift_lon(i), "lat": lat} for i in range(1, NLON)]
     peers += [{"lon": lon, "lat": shift_lat(i)} for i in range(1, NLAT)]
-    peers += [device(x, (y + i) % 4, z, core) for i in (1, 3)]
+    peers += [plane_peer(i, j) for i in range(4) for j in range(4) if i or j]
     peers += [{"lon": shift_lon(i), "lat": shift_lat(j)} for i in (-1, 1) for j in (-1, 1)]
     for peer in peers:
         pl.semaphore_signal(barrier, inc=1, device_id=peer, device_id_type=MESH)
@@ -136,6 +143,7 @@
 
     for copy in small:
         copy.wait()
+    cn_in.start()
 
     columns = [jnp.zeros((TLAT, TLON), F32) for _ in range(FIELDS)]
     cell_row, cell_col = cells[...] >> 7, cells[...] & 127
@@ -154,6 +162,8 @@
     for t in range(FIELDS):
         area[t, 8 : 8 + TLAT, :] = columns[t]
 
+    ens_in.start()
+
     area[5, 8 : 8 + TLAT, :] = ce[0]
     area[6, 8 : 8 + TLAT, :] = cn[0, 8 : 8 + TLAT, :]
     first = jnp.zeros((TLAT, TLON), F32)
@@ -176,12 +186,12 @@
     edges = [
         remote(area.at[:, pl.ds(TLAT, 8), :], area.at[:, low8, :], north),
         remote(area.at[:, pl.ds(8, 8), :], area.at[:, high8, :], south),
+        remote(pack_e, halo_w.at[mid, :], east),
+        remote(pack_w, halo_e.at[mid, :], west),
         remote(pack_e.at[pl.ds(TLAT - 8, 8), :], halo_w.at[low8, :], {"lon": shift_lon(1), "lat": shift_lat(1)}),
         remote(pack_e.at[pl.ds(0, 8), :], halo_w.at[high8, :], {"lon": shift_lon(1), "lat": shift_lat(-1)}),
         remote(pack_w.at[pl.ds(TLAT - 8, 8), :], halo_e.at[low8, :], {"lon": shift_lon(-1), "lat": shift_lat(1)}),
         remote(pack_w.at[pl.ds(0, 8), :], halo_e.at[high8, :], {"lon": shift_lon(-1), "lat": shift_lat(-1)}),
-        remote(pack_e, halo_w.at[mid, :], east),
-        remote(pack_w, halo_e.at[mid, :], west),
     ]
     for copy in edges:
         copy.start()
@@ -242,107 +252,14 @@
     for copy in routes:
         copy.start()
 
-    for copy in edges:
+    for copy in edges[:4]:
         copy.wait_recv()
-
-    wide_lane = iota((ROWS, TLON), 1)
-
-    def widened(n):
-        from_east = halo_e[...] if n == 0 else pltpu.roll(halo_e[...], 128 - 4 * n, 1)
-        from_west = pltpu.roll(halo_w[...], 124 - 4 * n, 1)
-        side = jnp.where(wide_lane < 64, from_east, from_west)
-        return jnp.concatenate([area[n], side], axis=1)
-
-    def up(v, axis):
-        return pltpu.roll(v, v.shape[axis] - 1, axis)
-
-    def down(v, axis):
-        return pltpu.roll(v, 1, axis)
-
-    forced = [widened(t) for t in range(FIELDS)]
-    east0 = widened(5)
-    global_row = lat * TLAT - 8 + iota((ROWS, 2 * TLON), 0)
-    inside = (global_row >= 0) & (global_row < NLAT * TLAT - 1)
-    north0 = jnp.where(inside, widened(6), 0.0)
-    pe0, pn0 = jnp.maximum(east0, 0.0), jnp.maximum(north0, 0.0)
-    aw0, as0 = -jnp.minimum(down(east0, 1), 0.0), -jnp.minimum(down(north0, 0), 0.0)
-    c00 = 1.0 - pe0 - aw0 - pn0 - as0
-    k0 = kern[0]
-    level = k0 * forced[0]
-    surface_wide = level
-    for t in range(1, FIELDS):
-        level = (
-            c00 * level + pe0 * up(level, 1) + aw0 * down(level, 1)
-            + pn0 * up(level, 0) + as0 * down(level, 0) + k0 * forced[t]
-        )
-        surface_wide = surface_wide + level
-    surface = surface_wide[8 : 8 + TLAT, :TLON]
-    prior[...] = surface
-    base = forced[0]
-    for n, v in enumerate((base, up(base, 1), down(base, 1), up(base, 0), down(base, 0))):
-        shifted[n] = v[8 : 8 + TLAT, :TLON]
-
-    ens_in.wait()
-    rounded = surface.astype(BF16).astype(F32)
-
-    @pl.loop(0, MEM)
-    def _(m):
-        product = ens[m].astype(F32) * rounded
-        for r in range(4):
-            at = pl.multiple_of((r * MEM + m) * 8, 8)
-            partial[pl.ds(at, 8), :] = product[r * 16 : r * 16 + 8] + product[r * 16 + 8 : r * 16 + 16]
-
-    row_sums = partial[pl.ds(0, 256, stride=8), :]
-    for s in range(1, 8):
-        row_sums += partial[pl.ds(s, 256, stride=8), :]
-    in_block = jnp.where(iota((8, TLON), 0) == iota((8, TLON), 1) // BLK, 1.0, 0.0).astype(BF16)
-    own[...] = sum(dot_nt(in_block, part) for part in parts_of(row_sums, 3))
-
-    slot = jnp.where(core == 0, z * 16 + y * 4 + x, x * 16 + z * 4 + y)
-    sibling = device(x, y, z, 1 - core)
-    moves = [(1 - core, core, 0), (0, 1 - core, core), (core, 0, 1 - core)]
-
-    def ring_peer(phase, s):
-        dx, dy, dz = moves[phase]
-        return device((x + s * dx) % 4, (y + s * dy) % 4, (z + s * dz) % 4, core)
-
-    def gather_sends(phase):
-        if phase == 0:
-            src, dst = own, table.at[core, slot]
-        else:
-            size = 4**phase
-            first_slot = slot // size * size
-            src = table.at[core, pl.ds(first_slot, size)]
-            dst = table.at[core, pl.ds(first_slot, size)]
-        return [remote(src, dst, ring_peer(phase, s)) for s in (2, 1, 3)]
-
-    def share_sends(phase):
-        size = 4**phase
-        group = slot // (4 * size) * (4 * size)
-        place = slot // size % 4
-        copies = []
-        for s in (1, 3, 2):
-            rows = pl.ds(group + (place + s) % 4 * size, size)
-            copies.append(remote(table.at[core, rows], table.at[core, rows], sibling))
-        return copies
-
-    shares = [remote(own, table.at[core, slot], sibling)]
-    gathers = [gather_sends(0)]
-    for copy in gathers[0] + shares:
-        copy.start()
-    table[core, slot] = own[...]
-
-    def next_phase(phase):
-        for copy in gathers[phase]:
-            copy.wait_recv()
-        if phase < 2:
-            gathers.append(gather_sends(phase + 1))
-            for copy in gathers[phase + 1]:
-                copy.start()
-        more = share_sends(phase)
-        for copy in more:
-            copy.start()
-        shares.extend(more)
+    base = area[0, 8 : 8 + TLAT, :]
+    shifted[0] = base
+    shifted[1] = jnp.where(lane == 127, pltpu.roll(halo_e[8 : 8 + TLAT, :], 127, 1), pltpu.roll(base, 127, 1))
+    shifted[2] = jnp.where(lane == 0, pltpu.roll(halo_w[8 : 8 + TLAT, :], 125, 1), pltpu.roll(base, 1, 1))
+    shifted[3] = area[0, 9 : 9 + TLAT, :]
+    shifted[4] = area[0, 7 : 7 + TLAT, :]
 
     for copy in courants:
         copy.wait_recv()
@@ -406,7 +323,7 @@
     sent = {}
     outs = []
 
-    def run_group(t, g):
+    def run_group(t, g, share=None):
         start = g * KG * ROWS
         halo = chalo[...]
         if t > 1:
@@ -415,8 +332,9 @@
             field_rows[pl.ds(start + 7, KG, stride=ROWS), :] = frhalo_s[t - 2, g]
             field_rows[pl.ds(start + 8 + TLAT, KG, stride=ROWS), :] = frhalo_n[t - 2, g]
             halo = jnp.where(lane < 32, fhalo_w[t - 2, g], fhalo_e[t - 2, g])
-        run = functools.partial(block, t, g, halo)
-        pack = lax.fori_loop(0, KG // LEVELS, run, 0 if t == 4 else jnp.zeros((TLAT, TLON), F32))
+        if share is not None:
+            add_weights(share, 0)
+        pack = block(t, g, halo, 0, jnp.zeros((TLAT, TLON), F32))
         if t == 4:
             levels = pl.ds(g * KG, KG)
             outs.append(pltpu.make_async_copy(last.at[levels], out_hbm.at[levels], out_sem.at[g]))
@@ -435,6 +353,8 @@
             copy.start()
 
     run_group(1, 0)
+    run_group(1, 1)
+    run_group(1, 2)
 
     route1[lon] = slots1[lon]
     for copy in routes:
@@ -450,14 +370,92 @@
         copy.start()
     route2[lat] = slots2[lat]
 
-    run_group(1, 1)
-    next_phase(0)
-    run_group(1, 2)
+    for copy in edges[4:]:
+        copy.wait_recv()
+
+    wide_lane = iota((ROWS, TLON), 1)
+
+    def widened(n):
+        from_east = halo_e[...] if n == 0 else pltpu.roll(halo_e[...], 128 - 4 * n, 1)
+        from_west = pltpu.roll(halo_w[...], 124 - 4 * n, 1)
+        side = jnp.where(wide_lane < 64, from_east, from_west)
+        return jnp.concatenate([area[n], side], axis=1)
+
+    def up(v, axis):
+        return pltpu.roll(v, v.shape[axis] - 1, axis)
+
+    def down(v, axis):
+        return pltpu.roll(v, 1, axis)
+
+    forced = [widened(t) for t in range(FIELDS)]
+    east0 = widened(5)
+    global_row = lat * TLAT - 8 + iota((ROWS, 2 * TLON), 0)
+    inside = (global_row >= 0) & (global_row < NLAT * TLAT - 1)
+    north0 = jnp.where(inside, widened(6), 0.0)
+    pe0, pn0 = jnp.maximum(east0, 0.0), jnp.maximum(north0, 0.0)
+    aw0, as0 = -jnp.minimum(down(east0, 1), 0.0), -jnp.minimum(down(north0, 0), 0.0)
+    c00 = 1.0 - pe0 - aw0 - pn0 - as0
+    k0 = kern[0]
+    level = k0 * forced[0]
+    surface_wide = level
+    for t in range(1, FIELDS):
+        level = (
+            c00 * level + pe0 * up(level, 1) + aw0 * down(level, 1)
+            + pn0 * up(level, 0) + as0 * down(level, 0) + k0 * forced[t]
+        )
+        surface_wide = surface_wide + level
+    surface = surface_wide[8 : 8 + TLAT, :TLON]
+    prior[...] = surface
+
+    ens_in.wait()
+    rounded = surface.astype(BF16).astype(F32)
+
+    @pl.loop(0, MEM)
+    def _(m):
+        product = ens[m].astype(F32) * rounded
+        for r in range(4):
+            at = pl.multiple_of((r * MEM + m) * 8, 8)
+            partial[pl.ds(at, 8), :] = product[r * 16 : r * 16 + 8] + product[r * 16 + 8 : r * 16 + 16]
+
+    row_sums = partial[pl.ds(0, 256, stride=8), :]
+    for s in range(1, 8):
+        row_sums += partial[pl.ds(s, 256, stride=8), :]
+    in_block = jnp.where(iota((8, TLON), 0) == iota((8, TLON), 1) // BLK, 1.0, 0.0).astype(BF16)
+    own[...] = sum(dot_nt(in_block, part) for part in parts_of(row_sums, 3))
+
+    slot = jnp.where(core == 0, z * 16 + y * 4 + x, x * 16 + z * 4 + y)
+    sibling = device(x, y, z, 1 - core)
+    group = pl.ds(slot // 16 * 16, 16)
+    plane = [
+        remote(own, table.at[core, slot], plane_peer(i, j))
+        for i in (2, 1, 3, 0) for j in (2, 1, 3, 0) if i or j
+    ]
+    for copy in plane:
+        copy.start()
+    table[core, slot] = own[...]
+    shares, line = [], []
+
+    def gather_line():
+        for copy in plane:
+            copy.wait_recv()
+        line.extend(remote(table.at[core, group], table.at[core, group], line_peer(i)) for i in (2, 1, 3))
+        shares.append(remote(table.at[core, group], table.at[core, group], sibling))
+        for copy in line + shares:
+            copy.start()
+
+    def share_line():
+        for n, i in enumerate((1, 3, 2)):
+            line[(1, 2, 0)[n]].wait_recv()
+            rows = pl.ds((slot // 16 + (4 - i)) % 4 * 16, 16)
+            copy = remote(table.at[core, rows], table.at[core, rows], sibling)
+            copy.start()
+            shares.append(copy)
 
     run_group(2, 0)
     run_group(2, 1)
-    next_phase(1)
     run_group(2, 2)
+
+    gather_line()
 
     for copy in routes2:
         copy.wait_recv()
@@ -471,7 +469,7 @@
     weights[...] = jnp.zeros_like(weights)
 
     def add_weights(i, carry):
-        at = pl.ds(pl.multiple_of(i * 8, 8), 8)
+        at = pl.ds(i * 8 if isinstance(i, int) else pl.multiple_of(i * 8, 8), 8)
         key1, key2, weight = keys[0, at, :].astype(I32), keys[1, at, :].astype(I32), keys[2, at, :]
         number = iota((128, 128), 0).astype(I16)
         lhs, rhs = [], []
@@ -484,19 +482,20 @@
         weights[...] += dot_nt(jnp.concatenate(lhs, axis=1), jnp.concatenate(rhs, axis=1))
         return carry
 
-    lax.fori_loop(0, 4, add_weights, 0)
-
-    run_group(3, 0)
-    run_group(3, 1)
-    next_phase(2)
-    run_group(3, 2)
-
-    lax.fori_loop(4, 8, add_weights, 0)
+    lax.fori_loop(0, 2, add_weights, 0)
+
+    run_group(3, 0, 2)
+    run_group(3, 1, 3)
+    run_group(3, 2, 4)
+
+    run_group(4, 0, 5)
+    share_line()
+    run_group(4, 1, 6)
+    run_group(4, 2, 7)
+
     w_parts = parts_of(weights[...], 2)
     weights16[0] = w_parts[0]
     weights16[1] = w_parts[1]
-
-    run_group(4, 0)
 
     for copy in shares:
         copy.wait_recv()
@@ -521,13 +520,9 @@
     outs.append(pltpu.make_async_copy(prior, prior_hbm, out_sem.at[GROUPS]))
     outs[-1].start()
 
-    run_group(4, 1)
-    run_group(4, 2)
-
     for copy in outs:
         copy.wait()
-    flights = edges + courants + routes + routes2 + shares
-    flights += [copy for group in gathers for copy in group]
+    flights = edges + courants + routes + routes2 + plane + line + shares
     flights += [copy for group in sent.values() for copy in group]
     for copy in flights:
         copy.wait_send()

time: 42.5 us -> 42.5 us (level)
  the two profiles are of different devices: /device:TPU:0 before, /device:TPU:1 now
where the time goes in v3:
time: 42.5 us; the launch traced here: 42.3 us
  Pallas kernels  41.7 us (98%)
  between operations  0.64 us (2%)
    pallas_call x1, Pallas kernels, per_device(): pl.pallas_call(kernel, out_shape=(jax.ShapeDtypeStruct((LEV,) + tile, F32...  39.2 us
    pallas_call x1, Pallas kernels, per_device(): pl.pallas_call(hand_over, out_shape=(jax.ShapeDtypeStruct((LEV,) + tile,...  2.53 us

profile of v3, /device:TPU:1, one launch (start us, length us, event | category | flops | bytes accessed | tf_op | source)
XLA Modules:
  0.0 42.3 jit_solution(17459850272294204505)
XLA Ops:
  0.6 39.2 %shard_map.113 = (f32[72,64,128]{2,1,0:T(8,128)}, f32[64,128]{1,0:T(8,128)}) custom-call(f32[72,64,128]{2,1,0:T(8,128)} %ce_hbm.1, f32[72,64,128]{2,1,0:T(8,128)} %cn_hbm.1, s32[8,128]{1,0:T(8,128)} %bitcast.6, f32[5,8,128]{2,1,0:T(8,128)} %bitcast.5, f32[72]{0:T(128)} %kern_hbm.1, bf16[64,64,128]{2,1,0:T(8,128)(2,1)} %ens_hbm.1, s32[8,128]{1,0:T(8,128)} %bitcast.7, ...), custom_call_target="tpu_custom_call" | custom-call | tf_op jit(solution)/shard_map/pallas_call | solution.py:555
  39.8 2.5 %shard_map.114 = (f32[72,64,128]{2,1,0:T(8,128)}, f32[64,128]{1,0:T(8,128)}) custom-call(f32[72,64,128]{2,1,0:T(8,128)} %get-tuple-element.4.field, f32[64,128]{1,0:T(8,128)} %get-tuple-element.5.prior), custom_call_target="tpu_custom_call" | custom-call | tf_op jit(solution)/shard_map/pallas_call | solution.py:620

commit v4 on v3

--- a/solution.py
+++ b/solution.py
@@ -137,8 +137,9 @@
     end = ((row % 128 == 127) & (col % 128 < 32)) | ((row % 128 == 0) & (col % 128 >= 32) & (col % 128 < 64))
     end = end & (row // 128 == col // 128)
     ends[...] = jnp.where(end, 1.0, 0.0).astype(BF16)
-    row, col = iota((128, 128), 0), iota((128, 128), 1)
-    every[...] = jnp.where(row == 127, 1.0, 0.0).astype(BF16)
+    end = (row % 128 == 127) & (row // 128 == col // 128)
+    every[...] = jnp.where(end, 1.0, 0.0).astype(BF16)
+    col = iota((128, 128), 1)
     to_first[...] = jnp.where(col == 0, 1.0, 0.0).astype(BF16)
 
     for copy in small:
@@ -198,14 +199,15 @@
 
     ce_in.wait()
 
-    def pack_courant(kb, acc):
-        faces = [ce[kb * 8 + i].astype(BF16) for i in range(8)]
-        tips = dot_nn(jnp.concatenate(faces, axis=0), every[...])
-        for i in range(8):
-            acc = jnp.where(lane == kb * 8 + i, tips[i * TLAT : (i + 1) * TLAT], acc)
-        return acc
-
-    cpack[...] = lax.fori_loop(0, LEV // 8, pack_courant, jnp.zeros((TLAT, TLON), F32))
+    tip_columns = jnp.zeros((TLAT, TLON), F32)
+    for k in range(0, LEV, KG):
+        faces = [ce[k + i].astype(BF16) for i in range(KG)]
+        pairs = [jnp.concatenate(faces[i : i + 2], axis=1) for i in range(0, KG, 2)]
+        tips = dot_nn(jnp.concatenate(pairs, axis=0), every[...])
+        for i in range(KG):
+            tip = tips[i // 2 * TLAT : (i // 2 + 1) * TLAT, i % 2 * TLON : (i % 2 + 1) * TLON]
+            tip_columns = jnp.where(lane == k + i, tip, tip_columns)
+    cpack[...] = tip_columns
     cn_in.wait()
     cn_rows = cn.reshape(LEV * (TLAT + 8), TLON)
     last_row = cn_rows[pl.ds(TLAT + 7, LEV, stride=TLAT + 8), :] * jnp.where(lat < NLAT - 1, 1.0, 0.0)
@@ -323,7 +325,7 @@
     sent = {}
     outs = []
 
-    def run_group(t, g, share=None):
+    def run_group(t, g):
         start = g * KG * ROWS
         halo = chalo[...]
         if t > 1:
@@ -332,8 +334,6 @@
             field_rows[pl.ds(start + 7, KG, stride=ROWS), :] = frhalo_s[t - 2, g]
             field_rows[pl.ds(start + 8 + TLAT, KG, stride=ROWS), :] = frhalo_n[t - 2, g]
             halo = jnp.where(lane < 32, fhalo_w[t - 2, g], fhalo_e[t - 2, g])
-        if share is not None:
-            add_weights(share, 0)
         pack = block(t, g, halo, 0, jnp.zeros((TLAT, TLON), F32))
         if t == 4:
             levels = pl.ds(g * KG, KG)
@@ -354,8 +354,6 @@
 
     run_group(1, 0)
     run_group(1, 1)
-    run_group(1, 2)
-
     route1[lon] = slots1[lon]
     for copy in routes:
         copy.wait_recv()
@@ -451,11 +449,11 @@
             copy.start()
             shares.append(copy)
 
+    run_group(1, 2)
+
     run_group(2, 0)
     run_group(2, 1)
     run_group(2, 2)
-
-    gather_line()
 
     for copy in routes2:
         copy.wait_recv()
@@ -469,7 +467,7 @@
     weights[...] = jnp.zeros_like(weights)
 
     def add_weights(i, carry):
-        at = pl.ds(i * 8 if isinstance(i, int) else pl.multiple_of(i * 8, 8), 8)
+        at = pl.ds(pl.multiple_of(i * 8, 8), 8)
         key1, key2, weight = keys[0, at, :].astype(I32), keys[1, at, :].astype(I32), keys[2, at, :]
         number = iota((128, 128), 0).astype(I16)
         lhs, rhs = [], []
@@ -482,30 +480,33 @@
         weights[...] += dot_nt(jnp.concatenate(lhs, axis=1), jnp.concatenate(rhs, axis=1))
         return carry
 
-    lax.fori_loop(0, 2, add_weights, 0)
-
-    run_group(3, 0, 2)
-    run_group(3, 1, 3)
-    run_group(3, 2, 4)
-
-    run_group(4, 0, 5)
-    share_line()
-    run_group(4, 1, 6)
-    run_group(4, 2, 7)
-
+    lax.fori_loop(0, 4, add_weights, 0)
+    gather_line()
+
+    run_group(3, 0)
+    run_group(3, 1)
+    run_group(3, 2)
+
+    lax.fori_loop(4, 8, add_weights, 0)
     w_parts = parts_of(weights[...], 2)
     weights16[0] = w_parts[0]
     weights16[1] = w_parts[1]
 
-    for copy in shares:
-        copy.wait_recv()
+    run_group(4, 0)
+    share_line()
+    run_group(4, 1)
+    run_group(4, 2)
+
     combined4 = jnp.zeros((128, 256), F32)
-    for q in range(4):
-        table_part = table[q // 2, (q % 2) * 32 : (q % 2) * 32 + 32].reshape(256, 256)
-        t_high, t_low = parts_of(table_part, 2)
-        w_rows, w_cols = slice(q // 2 * 128, q // 2 * 128 + 128), slice(q % 2 * 256, q % 2 * 256 + 256)
-        w_high, w_low = weights16[0, w_rows, w_cols], weights16[1, w_rows, w_cols]
-        combined4 += dot_nn(w_high, t_high) + dot_nn(w_high, t_low) + dot_nn(w_low, t_high)
+    for half in (core, 1 - core):
+        if half is not core:
+            for copy in shares:
+                copy.wait_recv()
+        for q in range(2):
+            t_high, t_low = parts_of(table[half, q * 32 : q * 32 + 32].reshape(256, 256), 2)
+            w_rows = pl.ds(pl.multiple_of(half * 128, 128), 128)
+            w_high, w_low = (weights16[n, w_rows, q * 256 : q * 256 + 256] for n in range(2))
+            combined4 += dot_nn(w_high, t_high) + dot_nn(w_high, t_low) + dot_nn(w_low, t_high)
     combined = combined4[:32, :64]
     for r in range(1, 4):
         combined += combined4[r * 32 : (r + 1) * 32, r * 64 : (r + 1) * 64]
@@ -589,8 +590,8 @@
             pltpu.VMEM((5,) + tile, F32),
         ]
         + [pltpu.VMEM((ROUNDS, GROUPS) + tile, F32) for _ in range(3)]
-        + [pltpu.VMEM((256, 256), BF16) for _ in range(2)]
-        + [pltpu.VMEM((128, 128), BF16) for _ in range(2)]
+        + [pltpu.VMEM((256, 256), BF16) for _ in range(3)]
+        + [pltpu.VMEM((128, 128), BF16)]
         + [pltpu.VMEM((ROUNDS, GROUPS, KG, TLON), F32) for _ in range(4)]
         + [
             pltpu.VMEM((NLON, 2, 8, 128), F32),

time: 42.5 us -> 43.3 us (1.019)
  Pallas kernels: 41.7 us -> 42.4 us
    pallas_call x1, Pallas kernels: 39.2 us -> 39.8 us  [per_device(): pl.pallas_call(kernel, out_shape=(jax.ShapeDtypeStruct((LEV,) + tile, F32...]
where the time goes in v4:
time: 43.3 us; the launch traced here: 43.2 us
  Pallas kernels  42.4 us (98%)
  between operations  0.8 us (2%)
    pallas_call x1, Pallas kernels, per_device(): pl.pallas_call(kernel, out_shape=(jax.ShapeDtypeStruct((LEV,) + tile, F32...  39.8 us
    pallas_call x1, Pallas kernels, per_device(): pl.pallas_call(hand_over, out_shape=(jax.ShapeDtypeStruct((LEV,) + tile,...  2.53 us

profile of v4, /device:TPU:1, one launch (start us, length us, event | category | flops | bytes accessed | tf_op | source)
XLA Modules:
  0.0 43.2 jit_solution(10862388677337695105)
XLA Ops:
  0.6 39.8 %shard_map.113 = (f32[72,64,128]{2,1,0:T(8,128)}, f32[64,128]{1,0:T(8,128)}) custom-call(f32[72,64,128]{2,1,0:T(8,128)} %ce_hbm.1, f32[72,64,128]{2,1,0:T(8,128)} %cn_hbm.1, s32[8,128]{1,0:T(8,128)} %bitcast.6, f32[5,8,128]{2,1,0:T(8,128)} %bitcast.5, f32[72]{0:T(128)} %kern_hbm.1, bf16[64,64,128]{2,1,0:T(8,128)(2,1)} %ens_hbm.1, s32[8,128]{1,0:T(8,128)} %bitcast.7, ...), custom_call_target="tpu_custom_call" | custom-call | tf_op jit(solution)/shard_map/pallas_call | solution.py:556
  40.5 2.5 %shard_map.114 = (f32[72,64,128]{2,1,0:T(8,128)}, f32[64,128]{1,0:T(8,128)}) custom-call(f32[72,64,128]{2,1,0:T(8,128)} %get-tuple-element.4.field, f32[64,128]{1,0:T(8,128)} %get-tuple-element.5.prior), custom_call_target="tpu_custom_call" | custom-call | tf_op jit(solution)/shard_map/pallas_call | solution.py:621

commit v5 on v4

--- a/solution.py
+++ b/solution.py
@@ -129,18 +129,6 @@
 
     lane = iota((TLAT, TLON), 1)
     lane32 = lane % 32
-
-    row, col = iota((256, 256), 0), iota((256, 256), 1)
-    shift = (row < 128) & (((col < 128) & (row == col + 1)) | ((col >= 128) & (row + 129 == col)))
-    edge = ((row >= 160) & (row < 192) & (col == 127)) | ((row >= 128) & (row < 160) & (col == 128))
-    move[...] = jnp.where(shift | edge, 1.0, 0.0).astype(BF16)
-    end = ((row % 128 == 127) & (col % 128 < 32)) | ((row % 128 == 0) & (col % 128 >= 32) & (col % 128 < 64))
-    end = end & (row // 128 == col // 128)
-    ends[...] = jnp.where(end, 1.0, 0.0).astype(BF16)
-    end = (row % 128 == 127) & (row // 128 == col // 128)
-    every[...] = jnp.where(end, 1.0, 0.0).astype(BF16)
-    col = iota((128, 128), 1)
-    to_first[...] = jnp.where(col == 0, 1.0, 0.0).astype(BF16)
 
     for copy in small:
         copy.wait()
@@ -197,6 +185,9 @@
     for copy in edges:
         copy.start()
 
+    row, col = iota((256, 256), 0), iota((256, 256), 1)
+    end = (row % 128 == 127) & (row // 128 == col // 128)
+    every[...] = jnp.where(end, 1.0, 0.0).astype(BF16)
     ce_in.wait()
 
     tip_columns = jnp.zeros((TLAT, TLON), F32)
@@ -253,6 +244,16 @@
     ]
     for copy in routes:
         copy.start()
+
+    row, col = iota((256, 256), 0), iota((256, 256), 1)
+    shift = (row < 128) & (((col < 128) & (row == col + 1)) | ((col >= 128) & (row + 129 == col)))
+    edge = ((row >= 160) & (row < 192) & (col == 127)) | ((row >= 128) & (row < 160) & (col == 128))
+    move[...] = jnp.where(shift | edge, 1.0, 0.0).astype(BF16)
+    end = ((row % 128 == 127) & (col % 128 < 32)) | ((row % 128 == 0) & (col % 128 >= 32) & (col % 128 < 64))
+    end = end & (row // 128 == col // 128)
+    ends[...] = jnp.where(end, 1.0, 0.0).astype(BF16)
+    col = iota((128, 128), 1)
+    to_first[...] = jnp.where(col == 0, 1.0, 0.0).astype(BF16)
 
     for copy in edges[:4]:
         copy.wait_recv()
@@ -354,6 +355,8 @@
 
     run_group(1, 0)
     run_group(1, 1)
+    run_group(1, 2)
+
     route1[lon] = slots1[lon]
     for copy in routes:
         copy.wait_recv()
@@ -448,8 +451,6 @@
             copy = remote(table.at[core, rows], table.at[core, rows], sibling)
             copy.start()
             shares.append(copy)
-
-    run_group(1, 2)
 
     run_group(2, 0)
     run_group(2, 1)

time: 43.3 us -> 42.9 us (level)
  no operation moved by 1% of the time
where the time goes in v5:
time: 42.9 us; the launch traced here: 42.8 us
  Pallas kernels  42 us (98%)
  between operations  0.8 us (2%)
    pallas_call x1, Pallas kernels, per_device(): pl.pallas_call(kernel, out_shape=(jax.ShapeDtypeStruct((LEV,) + tile, F32...  39.4 us
    pallas_call x1, Pallas kernels, per_device(): pl.pallas_call(hand_over, out_shape=(jax.ShapeDtypeStruct((LEV,) + tile,...  2.53 us

profile of v5, /device:TPU:1, one launch (start us, length us, event | category | flops | bytes accessed | tf_op | source)
XLA Modules:
  0.0 42.8 jit_solution(617927789668597496)
XLA Ops:
  0.6 39.4 %shard_map.113 = (f32[72,64,128]{2,1,0:T(8,128)}, f32[64,128]{1,0:T(8,128)}) custom-call(f32[72,64,128]{2,1,0:T(8,128)} %ce_hbm.1, f32[72,64,128]{2,1,0:T(8,128)} %cn_hbm.1, s32[8,128]{1,0:T(8,128)} %bitcast.6, f32[5,8,128]{2,1,0:T(8,128)} %bitcast.5, f32[72]{0:T(128)} %kern_hbm.1, bf16[64,64,128]{2,1,0:T(8,128)(2,1)} %ens_hbm.1, s32[8,128]{1,0:T(8,128)} %bitcast.7, ...), custom_call_target="tpu_custom_call" | custom-call | tf_op jit(solution)/shard_map/pallas_call | solution.py:557
  40.1 2.5 %shard_map.114 = (f32[72,64,128]{2,1,0:T(8,128)}, f32[64,128]{1,0:T(8,128)}) custom-call(f32[72,64,128]{2,1,0:T(8,128)} %get-tuple-element.4.field, f32[64,128]{1,0:T(8,128)} %get-tuple-element.5.prior), custom_call_target="tpu_custom_call" | custom-call | tf_op jit(solution)/shard_map/pallas_call | solution.py:622
